TPU v7x, 32 devices: a whole 2x2x4 slice. The times are simulated.
32 devices in a mesh: clip: 8 (over z, y), frame: 4 (over x, core).
Axes of the slice: x: 2, y: 2, z: 4, core: 2. Of those that a mesh axis runs over, the one named last changes fastest.
Arguments:
- video_tokens: bfloat16 [8, 8, 196, 768], P('clip', 'frame'), may hold values from -6 to 6
- time_gain: bfloat16 [768], P(('clip', 'frame')), may hold values from 0.25 to 1.75
- time_shift: bfloat16 [768], P(('clip', 'frame')), may hold values from -3 to 3
- time_inproj: bfloat16 [768, 2304], P(('clip', 'frame')), may hold values from -0.21875 to 0.21875
- time_inbias: bfloat16 [1536], P(('clip', 'frame')), may hold values from -3 to 3
- time_outproj: bfloat16 [768, 768], P(('clip', 'frame')), may hold values from -0.4375 to 0.4375
- time_outbias: bfloat16 [768], P(('clip', 'frame')), may hold values from -3 to 3
- time_linear: bfloat16 [768, 768], P(('clip', 'frame')), may hold values from -0.21875 to 0.21875
- time_linbias: bfloat16 [768], P(('clip', 'frame')), may hold values from -3 to 3
- space_gain: bfloat16 [768], P(('clip', 'frame')), may hold values from 0.25 to 1.75
- space_shift: bfloat16 [768], P(('clip', 'frame')), may hold values from -3 to 3
- space_inproj: bfloat16 [768, 2304], P(('clip', 'frame')), may hold values from -0.21875 to 0.21875
- space_inbias: bfloat16 [1536], P(('clip', 'frame')), may hold values from -3 to 3
- space_outproj: bfloat16 [768, 768], P(('clip', 'frame')), may hold values from -1.75 to 1.75
- space_outbias: bfloat16 [768], P(('clip', 'frame')), may hold values from -3 to 3
- feed_gain: bfloat16 [768], P(('clip', 'frame')), may hold values from 0.25 to 1.75
- feed_shift: bfloat16 [768], P(('clip', 'frame')), may hold values from -3 to 3
- expand_weight: bfloat16 [768, 3072], P(('clip', 'frame')), may hold values from -0.21875 to 0.21875
- expand_bias: bfloat16 [3072], P(('clip', 'frame')), may hold values from -3 to 3
- reduce_weight: bfloat16 [3072, 768], P(('clip', 'frame')), may hold values from -0.109375 to 0.109375
- reduce_bias: bfloat16 [768], P(('clip', 'frame')), may hold values from -3 to 3
- cotangent: bfloat16 [8, 8, 196, 768], P('clip', 'frame'), may hold values from -6 to 6
Outputs:
- layer_out: bfloat16 [8, 8, 196, 768], P('clip', 'frame')
- input_grad: float32 [8, 8, 196, 768], P('clip', 'frame')
- grad_time_gain: float32 [768], P(('clip', 'frame'))
- grad_time_shift: float32 [768], P(('clip', 'frame'))
- grad_time_inproj: float32 [768, 2304], P(('clip', 'frame'))
- grad_time_inbias: float32 [1536], P(('clip', 'frame'))
- grad_time_outproj: float32 [768, 768], P(('clip', 'frame'))
- grad_time_outbias: float32 [768], P(('clip', 'frame'))
- grad_time_linear: float32 [768, 768], P(('clip', 'frame'))
- grad_time_linbias: float32 [768], P(('clip', 'frame'))
- grad_space_gain: float32 [768], P(('clip', 'frame'))
- grad_space_shift: float32 [768], P(('clip', 'frame'))
- grad_space_inproj: float32 [768, 2304], P(('clip', 'frame'))
- grad_space_inbias: float32 [1536], P(('clip', 'frame'))
- grad_space_outproj: float32 [768, 768], P(('clip', 'frame'))
- grad_space_outbias: float32 [768], P(('clip', 'frame'))
- grad_feed_gain: float32 [768], P(('clip', 'frame'))
- grad_feed_shift: float32 [768], P(('clip', 'frame'))
- grad_expand_weight: float32 [768, 3072], P(('clip', 'frame'))
- grad_expand_bias: float32 [3072], P(('clip', 'frame'))
- grad_reduce_weight: float32 [3072, 768], P(('clip', 'frame'))
- grad_reduce_bias: float32 [768], P(('clip', 'frame'))
All inputs are finite; a program needn't handle non-finite values.
Results may differ from a plain program's by a relative error of at most 0.025.
Values may be sent and summed in bfloat16 or wider, within the bound.
A program may use at most 192 MiB of HBM per device.

v0:
```python
import functools

import jax
import jax.numpy as jnp
from jax import lax
from jax.experimental import pallas as pl
from jax.experimental.pallas import tpu as pltpu
from jax.sharding import PartitionSpec as P

LOW = jnp.bfloat16
WIDE = jnp.float32
HEADS = 12
norm_eps = 1e-06
LANES = 128
TILE = 256
T_GAIN, T_SHIFT, T_OUTB, T_LINB, S_GAIN, S_SHIFT, S_OUTB, F_GAIN, F_SHIFT, R_BIAS, T_INB, S_INB, E_BIAS = 0, 1, 2, 3, 4, 5, 6, 7, 8, 9, 10, 12, 14


def dot(a, b):
    return lax.dot_general(a, b, (((1,), (0,)), ((), ())), preferred_element_type=WIDE)


def dot_nt(a, b):
    return lax.dot_general(a, b, (((1,), (1,)), ((), ())), preferred_element_type=WIDE)


def each(count, act):
    def step(k, carry):
        act(k)
        return carry

    lax.fori_loop(0, count, step, 0)


def tiles(k, size=TILE):
    return pl.ds(pl.multiple_of(k * size, size), size)


def columns(w_ref, cut):
    block = w_ref[:, :, cut]
    return block.reshape((block.shape[0] * block.shape[1], block.shape[2]))


def normal(x):
    center = x - jnp.mean(x, axis=-1, keepdims=True)
    inverse = lax.rsqrt(jnp.mean(center * center, axis=-1, keepdims=True) + norm_eps)
    return center * inverse, inverse


def norm_stage(x_ref, vec, gain_row, a_ref, block):
    gain, shift = vec[gain_row : gain_row + 1, :], vec[gain_row + 1 : gain_row + 2, :]

    def act(k):
        rows = tiles(k, block)
        unit, _ = normal(x_ref[rows, :].astype(WIDE))
        a_ref[rows, :] = (unit * gain + shift).astype(LOW)

    each(x_ref.shape[0] // block, act)


def norm_back_stage(x_ref, vec, gain_row, da_ref, sums, block, store):
    gain = vec[gain_row : gain_row + 1, :]
    width = x_ref.shape[1]

    def step(k, carry):
        rows = tiles(k, block)
        unit, inverse = normal(x_ref[rows, :].astype(WIDE))
        da = da_ref[rows, :]
        e = da * gain
        dv = inverse * (
            e
            - jnp.mean(e, axis=-1, keepdims=True)
            - unit * jnp.mean(e * unit, axis=-1, keepdims=True)
        )
        store(rows, dv)
        grad_gain, grad_shift = carry
        fold = lambda v: jnp.sum(v.reshape(block // 8, 8, width), axis=0)
        return grad_gain + fold(da * unit), grad_shift + fold(da)

    zero = jnp.zeros((8, width), WIDE)
    grad_gain, grad_shift = lax.fori_loop(0, x_ref.shape[0] // block, step, (zero, zero))
    sums[gain_row : gain_row + 1, :] = jnp.sum(grad_gain, axis=0, keepdims=True)
    sums[gain_row + 1 : gain_row + 2, :] = jnp.sum(grad_shift, axis=0, keepdims=True)


def inproj_stage(a_ref, w_ref, vec, bias_row, z_ref):
    width = a_ref.shape[1]
    for part in range(3):

        def act(k, part=part):
            inner = tiles(k)
            cut = pl.ds(pl.multiple_of(part * width + k * TILE, TILE), TILE)
            total = dot(a_ref[...], columns(w_ref, cut))
            if part != 1:
                row = bias_row + part // 2
                total = total + vec[row : row + 1, inner]
            z_ref[:, cut] = total.astype(LOW)

        each(width // TILE, act)


def project_stage(a_ref, w_ref, vec, bias_row, store):
    def act(k):
        cut = tiles(k)
        store(cut, dot(a_ref[...], columns(w_ref, cut)) + vec[bias_row : bias_row + 1, cut])

    each(w_ref.shape[2] // TILE, act)


def back_stage(dz_ref, w_ref, acc_ref):
    width = acc_ref.shape[1]
    parts = w_ref.shape[2] // width
    acc_ref[...] = dot_nt(dz_ref[:, :width], columns(w_ref, pl.ds(0, width)))

    def act(k):
        cut = tiles(k + 1, width)
        acc_ref[...] = acc_ref[...] + dot_nt(dz_ref[:, cut], columns(w_ref, cut))

    if parts > 1:
        each(parts - 1, act)


def turn_stage(a_ref, at_ref):
    width = a_ref.shape[1]

    def act(k):
        at_ref[tiles(k), :] = a_ref[:, tiles(k)].T

    each(width // TILE, act)
    at_ref[width:, :] = jnp.ones((at_ref.shape[0] - width, at_ref.shape[1]), LOW)


def weight_stage(at_ref, dz_ref, g_ref, bias):
    depth, rows, _ = g_ref.shape
    full = depth * rows

    def act(k):
        cut = tiles(k)
        total = dot(at_ref[...], dz_ref[:, cut])
        g_ref[:, :, cut] = total[:full].astype(LOW).reshape((depth, rows, TILE))
        bias(k, total[full : full + 1])

    each(g_ref.shape[2] // TILE, act)


def bias_rows(sums, table, width):
    def act(k, total):
        per = width // TILE
        for part, row in enumerate(table):
            if row is None:
                continue

            @pl.when((k >= part * per) & (k < (part + 1) * per))
            def _():
                sums[row : row + 1, tiles(k - part * per)] = total

    return act


def low_head(rows):
    lane = lax.broadcasted_iota(jnp.int32, (rows, LANES), 1)
    return lane < LANES // 2


def space_attend(z_ref, p_ref, o_ref, frames, rows, valid, block):
    width = o_ref.shape[1]
    pairs = width // LANES
    scale = (LANES // 2) ** -0.5

    def act(step):
        f, pair = step // pairs, step % pairs
        span = tiles(f, rows)
        q = z_ref[span, pl.ds(pl.multiple_of(pair * LANES, LANES), LANES)]
        k = z_ref[span, pl.ds(pl.multiple_of(width + pair * LANES, LANES), LANES)]
        v = z_ref[span, pl.ds(pl.multiple_of(2 * width + pair * LANES, LANES), LANES)]
        first = low_head(rows)
        vt = v.T
        keep = lax.broadcasted_iota(jnp.int32, (rows, rows), 0) % block < valid
        outs = []
        for side in range(2):
            mine = first if side == 0 else ~first
            scores = dot_nt(k, jnp.where(mine, q, jnp.zeros_like(q))) * scale
            scores = jnp.where(keep, scores, -1e30)
            e = jnp.exp(scores - jnp.max(scores, axis=0, keepdims=True))
            p = (e * (1.0 / jnp.sum(e, axis=0, keepdims=True))).astype(LOW)
            p_ref[2 * step + side] = p
            outs.append(dot(vt, p))
        top = lax.broadcasted_iota(jnp.int32, (LANES, rows), 0) < LANES // 2
        o = jnp.where(top, outs[0], outs[1]).T
        o_ref[span, pl.ds(pl.multiple_of(pair * LANES, LANES), LANES)] = o.astype(LOW)

    each(frames * pairs, act)


def space_attend_back(z_ref, p_ref, do_ref, dz_ref, frames, rows):
    width = do_ref.shape[1]
    pairs = width // LANES
    scale = (LANES // 2) ** -0.5

    def act(step):
        f, pair = step // pairs, step % pairs
        span = tiles(f, rows)
        cut_q = pl.ds(pl.multiple_of(pair * LANES, LANES), LANES)
        cut_k = pl.ds(pl.multiple_of(width + pair * LANES, LANES), LANES)
        cut_v = pl.ds(pl.multiple_of(2 * width + pair * LANES, LANES), LANES)
        q, k, v, do = z_ref[span, cut_q], z_ref[span, cut_k], z_ref[span, cut_v], do_ref[span, cut_q]
        kt = k.T
        first = low_head(rows)
        dk = dv = None
        turned = []
        for side in range(2):
            mine = first if side == 0 else ~first
            q_side = jnp.where(mine, q, jnp.zeros_like(q))
            do_side = jnp.where(mine, do, jnp.zeros_like(do))
            p_low = p_ref[2 * step + side]
            p = p_low.astype(WIDE)
            dp = dot_nt(v, do_side)
            inner = jnp.sum(dp * p, axis=0, keepdims=True)
            ds = (p * (dp - inner)).astype(LOW)
            dv_side, dk_side = dot(p_low, do_side), dot(ds, q_side)
            dv = dv_side if dv is None else dv + dv_side
            dk = dk_side if dk is None else dk + dk_side
            turned.append(dot(kt, ds))
        top = lax.broadcasted_iota(jnp.int32, (LANES, rows), 0) < LANES // 2
        dq = jnp.where(top, turned[0], turned[1]).T
        dz_ref[span, cut_q] = (dq * scale).astype(LOW)
        dz_ref[span, cut_k] = (dk * scale).astype(LOW)
        dz_ref[span, cut_v] = dv.astype(LOW)

    each(frames * pairs, act)


def head_sum(width):
    row = lax.broadcasted_iota(jnp.int32, (width, LANES), 0) // (width // HEADS)
    col = lax.broadcasted_iota(jnp.int32, (width, LANES), 1)
    return (row == col).astype(WIDE).astype(LOW)


def head_spread(width):
    row = lax.broadcasted_iota(jnp.int32, (LANES, width), 0)
    col = lax.broadcasted_iota(jnp.int32, (LANES, width), 1) // (width // HEADS)
    return (row == col).astype(WIDE).astype(LOW)


def by_head(product, pick):
    high = product.astype(LOW)
    rest = (product - high.astype(WIDE)).astype(LOW)
    return dot(high, pick) + dot(rest, pick)


def time_attend(z_ref, p_ref, o_ref, frames, block):
    width = o_ref.shape[1]
    scale = (width // HEADS) ** -0.5
    pick, spread = head_sum(width), head_spread(width)
    spans = [slice(k * block, (k + 1) * block) for k in range(frames)]

    def act(pair):
        rows = tiles(pair, 2 * block)
        q = z_ref[rows, :width].astype(WIDE)
        scores = [[], []]
        for span in spans:
            k = z_ref[span, width : 2 * width].astype(WIDE)
            for half in range(2):
                scores[half].append(by_head(q[spans[half]] * k, pick) * scale)
        probs = []
        for half in range(2):
            top = functools.reduce(jnp.maximum, scores[half])
            e = [jnp.exp(s - top) for s in scores[half]]
            inverse = 1.0 / functools.reduce(jnp.add, e)
            probs.append([item * inverse for item in e])
        out = [jnp.zeros((block, width), WIDE)] * 2
        for k, span in enumerate(spans):
            v = z_ref[span, 2 * width :].astype(WIDE)
            for half in range(2):
                p = probs[half][k]
                p_ref[2 * pair + half, span, :] = p
                out[half] = out[half] + dot(p.astype(LOW), spread) * v
        o_ref[rows, :] = jnp.concatenate(out, axis=0).astype(LOW)

    each(frames // 2, act)


def time_attend_back(z_ref, p_ref, do_ref, dz_ref, dk_ref, dv_ref, frames, block):
    width = do_ref.shape[1]
    scale = (width // HEADS) ** -0.5
    pick, spread = head_sum(width), head_spread(width)
    spans = [slice(k * block, (k + 1) * block) for k in range(frames)]
    dk_ref[...] = jnp.zeros_like(dk_ref)
    dv_ref[...] = jnp.zeros_like(dv_ref)

    def act(pair):
        rows = tiles(pair, 2 * block)
        do = do_ref[rows, :].astype(WIDE)
        q = z_ref[rows, :width].astype(WIDE)
        dps = [[], []]
        inner = [jnp.zeros((block, LANES), WIDE)] * 2
        for span in spans:
            v = z_ref[span, 2 * width :].astype(WIDE)
            for half in range(2):
                dp = by_head(do[spans[half]] * v, pick)
                inner[half] = inner[half] + dp * p_ref[2 * pair + half, span, :]
                dps[half].append(dp)
        dq = [jnp.zeros((block, width), WIDE)] * 2
        for at, span in enumerate(spans):
            k = z_ref[span, width : 2 * width].astype(WIDE)
            dk, dv = dk_ref[span, :], dv_ref[span, :]
            for half in range(2):
                p = p_ref[2 * pair + half, span, :]
                ds = dot((p * (dps[half][at] - inner[half])).astype(LOW), spread)
                dq[half] = dq[half] + ds * k
                dk = dk + ds * q[spans[half]]
                dv = dv + dot(p.astype(LOW), spread) * do[spans[half]]
            dk_ref[span, :] = dk
            dv_ref[span, :] = dv
        dz_ref[rows, :width] = (jnp.concatenate(dq, axis=0) * scale).astype(LOW)

    each(frames // 2, act)

    def out(pair):
        rows = tiles(pair, 2 * block)
        dz_ref[rows, width : 2 * width] = (dk_ref[rows, :] * scale).astype(LOW)
        dz_ref[rows, 2 * width :] = dv_ref[rows, :].astype(LOW)

    each(frames // 2, out)


def expand_stage(a_ref, w_ref, vec, g_ref, slope_ref):
    width = a_ref.shape[1]
    per = width // TILE

    def act(k):
        cut = tiles(k)
        h = dot(a_ref[...], columns(w_ref, cut))
        inner = tiles(k % per)
        bias = vec[pl.ds(E_BIAS + k // per, 1), inner]
        h = h + bias
        cdf = 0.5 * (1.0 + lax.erf(h * (0.5 ** 0.5)))
        g_ref[:, cut] = (h * cdf).astype(LOW)
        slope_ref[:, cut] = (cdf + h * (jnp.exp(-0.5 * h * h) * 0.3989422804014327)).astype(LOW)

    each(w_ref.shape[2] // TILE, act)


def reduce_stage(g_ref, w_ref, vec, x_ref, out_store):
    depth, rows, width = w_ref.shape

    def act(k):
        cut = tiles(k)
        total = x_ref[:, cut] + vec[R_BIAS : R_BIAS + 1, cut]
        for z in range(depth):
            total = total + dot(g_ref[:, z * rows : (z + 1) * rows], w_ref[z, :, cut])
        out_store(cut, total)

    each(width // TILE, act)


def reduce_back_stage(dm_ref, w_ref, slope_ref, dh_ref):
    depth, rows, _ = w_ref.shape
    per = rows // TILE

    def act(k):
        cut = tiles(k)
        block = w_ref[k // per, tiles(k % per), :]
        dh_ref[:, cut] = (dot_nt(dm_ref[...], block) * slope_ref[:, cut].astype(WIDE)).astype(LOW)

    each(depth * per, act)


def reduce_grad_stage(g_ref, gt_ref, dm_ref, out_ref, sums):
    depth, rows, width = out_ref.shape

    def act(k):
        z, part = k // (rows // TILE), k % (rows // TILE)
        turned = g_ref[:, tiles(k)].T
        gt_ref[...] = turned
        out_ref[z, tiles(part), :] = dot(gt_ref[...], dm_ref[...]).astype(LOW)

    each(depth * rows // TILE, act)
    ones = jnp.ones((16, dm_ref.shape[0]), LOW)
    sums[R_BIAS : R_BIAS + 1, :] = dot(ones, dm_ref[...])[:1]


def vmem_call(body, outs, ins, scratch, name):
    return pl.pallas_call(
        body,
        out_shape=[jax.ShapeDtypeStruct(shape, kind) for shape, kind in outs],
        in_specs=[pl.BlockSpec(memory_space=pltpu.VMEM)] * len(ins),
        out_specs=[pl.BlockSpec(memory_space=pltpu.VMEM)] * len(outs),
        scratch_shapes=[pltpu.VMEM(shape, kind) for shape, kind in scratch],
        compiler_params=pltpu.CompilerParams(vmem_limit_bytes=60 << 20),
        name=name,
    )(*ins)


def time_forward(block, x, vec, w_in, w_out, w_lin):
    rows, width = x.shape
    frames = rows // block

    def body(x_ref, vec_ref, w_in, w_out, w_lin, b_ref, a_ref, z_ref, p_ref, o_ref, u_ref):
        def store(ref):
            def act(cut, total):
                ref[:, cut] = total.astype(LOW)

            return act

        norm_stage(x_ref, vec_ref, T_GAIN, a_ref, 2 * block)
        inproj_stage(a_ref, w_in, vec_ref, T_INB, z_ref)
        time_attend(z_ref, p_ref, o_ref, frames, block)
        project_stage(o_ref, w_out, vec_ref, T_OUTB, store(u_ref))
        project_stage(u_ref, w_lin, vec_ref, T_LINB, store(b_ref))

    token = ((rows, width), LOW)
    outs = [token, token, ((rows, 3 * width), LOW), ((frames, rows, LANES), WIDE), token, token]
    return vmem_call(body, outs, (x, vec, w_in, w_out, w_lin), [], "time_forward")


def space_layer(shape, x, b, dy, vec, w_in, w_out, w_up, w_down):
    frames, valid, block = shape
    rows, width = x.shape
    span = rows // frames
    hidden = w_up.shape[2]
    heads_all = frames * HEADS

    def body(x_ref, b_ref, dy_ref, vec_ref, w_in, w_out, w_up, w_down, out_ref, dx1_ref, db_ref,
             g_in, g_out, g_up, g_down, sums, x1, x2, a_s, z_s, p_s, o_s, a_m, act_g, slope, dh, acc, at, gt, low):
        sums[...] = jnp.zeros_like(sums)

        def first(k):
            r = tiles(k, 2 * block)
            x1[r, :] = x_ref[r, :].astype(WIDE) + b_ref[r, :].astype(WIDE)

        each(rows // (2 * block), first)
        norm_stage(x1, vec_ref, S_GAIN, a_s, 2 * block)
        inproj_stage(a_s, w_in, vec_ref, S_INB, z_s)
        space_attend(z_s, p_s, o_s, frames, span, valid, block)

        def add_x1(cut, total):
            x2[:, cut] = x1[:, cut] + total

        project_stage(o_s, w_out, vec_ref, S_OUTB, add_x1)
        norm_stage(x2, vec_ref, F_GAIN, a_m, 2 * block)
        expand_stage(a_m, w_up, vec_ref, act_g, slope)

        def put_out(cut, total):
            out_ref[:, cut] = total.astype(LOW)

        reduce_stage(act_g, w_down, vec_ref, x2, put_out)
        reduce_grad_stage(act_g, gt, dy_ref, g_down, sums)
        reduce_back_stage(dy_ref, w_down, slope, dh)
        turn_stage(a_m, at)
        weight_stage(at, dh, g_up, bias_rows(sums, [E_BIAS + k for k in range(hidden // width)], width))
        back_stage(dh, w_up, acc)

        def put_x2(r, dv):
            total = dy_ref[r, :].astype(WIDE) + dv
            dx1_ref[r, :] = total
            low[r, :] = total.astype(LOW)

        norm_back_stage(x2, vec_ref, F_GAIN, acc, sums, 2 * block, put_x2)
        turn_stage(o_s, at)
        weight_stage(at, low, g_out, bias_rows(sums, [S_OUTB], width))
        back_stage(low, w_out, acc)
        low[...] = acc[...].astype(LOW)
        dz = dh.at[:, : 3 * width]
        space_attend_back(z_s, p_s, low, dz, frames, span)
        turn_stage(a_s, at)
        weight_stage(at, dz, g_in, bias_rows(sums, [S_INB, None, S_INB + 1], width))
        back_stage(dz, w_in, acc)

        def put_x1(r, dv):
            total = dx1_ref[r, :] + dv
            dx1_ref[r, :] = total
            db_ref[r, :] = total.astype(LOW)

        norm_back_stage(x1, vec_ref, S_GAIN, acc, sums, 2 * block, put_x1)

    token, full = ((rows, width), LOW), ((rows, width), WIDE)
    outs = [token, full, token] + [(w.shape, LOW) for w in (w_in, w_out, w_up, w_down)] + [(vec.shape, WIDE)]
    scratch = [full, full, token, ((rows, 3 * width), LOW), ((heads_all, span, span), LOW), token, token]
    scratch += [((rows, hidden), LOW)] * 3 + [full, ((width + 16, rows), LOW), ((TILE, rows), LOW), token]
    return vmem_call(body, outs, (x, b, dy, vec, w_in, w_out, w_up, w_down), scratch, "space_layer")


def time_backward(block, db, x, a, z, p, o, u, vec, w_in, w_out, w_lin):
    rows, width = x.shape
    frames = rows // block

    def body(db_ref, x_ref, a_ref, z_ref, p_ref, o_ref, u_ref, vec_ref, w_in, w_out, w_lin,
             dt_ref, g_in, g_out, g_lin, sums, low, dz, dk, dv, acc, at):
        sums[...] = jnp.zeros_like(sums)
        turn_stage(u_ref, at)
        weight_stage(at, db_ref, g_lin, bias_rows(sums, [T_LINB], width))
        back_stage(db_ref, w_lin, acc)
        low[...] = acc[...].astype(LOW)
        turn_stage(o_ref, at)
        weight_stage(at, low, g_out, bias_rows(sums, [T_OUTB], width))
        back_stage(low, w_out, acc)
        low[...] = acc[...].astype(LOW)
        time_attend_back(z_ref, p_ref, low, dz, dk, dv, frames, block)
        turn_stage(a_ref, at)
        weight_stage(at, dz, g_in, bias_rows(sums, [T_INB, None, T_INB + 1], width))
        back_stage(dz, w_in, acc)

        def put(r, dv):
            dt_ref[r, :] = dv.astype(LOW)

        norm_back_stage(x_ref, vec_ref, T_GAIN, acc, sums, 2 * block, put)

    token, full = ((rows, width), LOW), ((rows, width), WIDE)
    outs = [token] + [(w.shape, LOW) for w in (w_in, w_out, w_lin)] + [(vec.shape, WIDE)]
    scratch = [token, ((rows, 3 * width), LOW), full, full, full, ((width + 16, rows), LOW)]
    return vmem_call(body, outs, (db, x, a, z, p, o, u, vec, w_in, w_out, w_lin), scratch, "time_backward")


def stack_rows(terms, groups):
    return tuple(
        (item.reshape((groups, item.shape[0] // groups) + item.shape[1:]) for item in terms)
    )


def fold_rows(received):
    return tuple((jnp.sum(item, axis=0) for item in received))


MESH = pl.DeviceIdType.MESH
TILE_ROWS = 8
SMALL_TILE = (8, 256)


def remote(source, target, send, recv, device):
    return pltpu.make_async_remote_copy(
        src_ref=source,
        dst_ref=target,
        send_sem=send,
        recv_sem=recv,
        device_id=device,
        device_id_type=MESH,
    )


def place(split):
    nz, ny, nx, nc = split
    clip, frame = lax.axis_index("clip"), lax.axis_index("frame")
    z, y, x, c = clip // ny, clip % ny, frame // nc, frame % nc

    def mesh_at(z, y, x, c):
        return (z * ny + y, x * nc + c)

    row = [mesh_at((z + step) % nz, y, x, c) for step in range(1, nz)]
    beside = (mesh_at(z, y, 1 - x, c), mesh_at(z, 1 - y, x, c), mesh_at(z, y, x, 1 - c))
    return (z, y, x, c), row, beside


def greet(devices):
    barrier = pltpu.get_barrier_semaphore()
    for device in devices:
        pl.semaphore_signal(barrier, inc=1, device_id=device, device_id_type=MESH)
    pl.semaphore_wait(barrier, len(devices))


def gather_kernel(split, count, *refs):
    shards, full = refs[:count], refs[count : 2 * count]
    row_send, row_recv, side_send, side_recv, core_send, core_recv, own_sem = refs[2 * count :]
    (z, y, x, c), row, (across_x, across_y, twin) = place(split)
    greet(row + [across_x, across_y, twin])
    started, first, second, third, core = [], {}, {}, {}, {}

    def launch(copy):
        copy.start()
        started.append(copy)
        return copy

    def to_twin(i, step, block):
        return launch(remote(block, block, core_send.at[i, step], core_recv.at[i, step], twin))

    def spread(i):
        own = full[i].at[z, y, x, c]
        first[i] = [
            launch(remote(shards[i], own, row_send.at[i, k], row_recv.at[i, k], device))
            for k, device in enumerate(row)
        ]
        keep = pltpu.make_async_copy(shards[i], own, own_sem.at[i])
        keep.start()
        first[i].append(keep)

    def sideways(i):
        for copy in first[i][:-1]:
            copy.wait_recv()
        first[i][-1].wait()
        block = full[i].at[:, y, x, c]
        second[i] = [
            launch(remote(block, block, side_send.at[i, k], side_recv.at[i, k], device))
            for k, device in enumerate((across_x, across_y))
        ]
        core[i] = [to_twin(i, 0, block)]

    def relay(i):
        half = shards[i].shape[-1] // 2
        second[i][0].wait_recv()
        part = full[i].at[:, y, 1 - x, c, :, pl.ds(0, half)]
        third[i] = [launch(remote(part, part, side_send.at[i, 2], side_recv.at[i, 2], across_y))]
        core[i].append(to_twin(i, 1, full[i].at[:, y, 1 - x, c]))
        second[i][1].wait_recv()
        part = full[i].at[:, 1 - y, x, c, :, pl.ds(half, half)]
        third[i].append(
            launch(remote(part, part, side_send.at[i, 3], side_recv.at[i, 3], across_x))
        )
        core[i].append(to_twin(i, 2, full[i].at[:, 1 - y, x, c]))

    def finish(i):
        for copy in third[i]:
            copy.wait_recv()
        core[i].append(to_twin(i, 3, full[i].at[:, 1 - y, 1 - x, c]))

    def receive(i):
        for copy in core[i]:
            copy.wait_recv()

    ahead = 2
    for i in range(min(ahead, count)):
        spread(i)
    for step in range(count + 3):
        for lag, act in enumerate((sideways, relay, finish, receive)):
            if 0 <= step - lag < count:
                act(step - lag)
            if lag == 0 and step + ahead < count:
                spread(step + ahead)
    for copy in started:
        copy.wait_send()


def gather_shards(split, shards):
    count = len(shards)
    sem = pltpu.SemaphoreType.DMA
    full = pl.pallas_call(
        functools.partial(gather_kernel, split, count),
        out_shape=[jax.ShapeDtypeStruct(split + item.shape, item.dtype) for item in shards],
        in_specs=[pl.BlockSpec(memory_space=pl.ANY)] * count,
        out_specs=[pl.BlockSpec(memory_space=pl.ANY)] * count,
        scratch_shapes=[sem((count, split[0] - 1))] * 2 + [sem((count, 4))] * 4 + [sem((count,))],
        compiler_params=pltpu.CompilerParams(collective_id=0, has_side_effects=True),
        name="gather_shards",
    )(*shards)
    return [item.reshape((-1, item.shape[-1])) for item in full]


def sum_kernel(split, count, *refs):
    groups = [refs[k * count : (k + 1) * count] for k in range(8)]
    mine, outs, held, low_half, high_half, from_x, from_y, from_row = groups
    core_send, core_recv, side_send, side_recv, row_send, row_recv = refs[8 * count :]
    (z, y, x, c), row, (across_x, across_y, twin) = place(split)
    greet(row + [across_x, across_y, twin])
    depth = split[0]
    started, core, diagonal, side, last = [], {}, {}, {}, {}

    def launch(copy):
        copy.start()
        started.append(copy)
        return copy

    def each_row(act):
        def step(k, carry):
            act(k)
            return carry

        lax.fori_loop(0, depth, step, 0)

    def swap(i):
        block = mine[i].at[:, :, :, 1 - c]
        core[i] = launch(remote(block, held[i], core_send.at[i], core_recv.at[i], twin))

    def fold_core(i):
        core[i].wait_recv()
        half = mine[i].shape[-1] // 2

        def fold(yy, xx):
            def act(k):
                held[i][k, yy, xx] = held[i][k, yy, xx] + mine[i][k, yy, xx, c]

            each_row(act)

        fold(1 - y, 1 - x)
        low = held[i].at[:, 1 - y, 1 - x, :, pl.ds(0, half)]
        high = held[i].at[:, 1 - y, 1 - x, :, pl.ds(half, half)]
        diagonal[i] = [
            launch(remote(low, low_half[i], side_send.at[i, 0], side_recv.at[i, 0], across_x)),
            launch(remote(high, high_half[i], side_send.at[i, 1], side_recv.at[i, 1], across_y)),
        ]
        fold(1 - y, x)
        fold(y, 1 - x)
        fold(y, x)

    def fold_diagonal(i):
        half = mine[i].shape[-1] // 2
        diagonal[i][0].wait_recv()

        def act_low(k):
            held[i][k, 1 - y, x, :, :half] = held[i][k, 1 - y, x, :, :half] + low_half[i][k]

        each_row(act_low)
        block = held[i].at[:, 1 - y, x]
        side[i] = [
            launch(remote(block, from_y[i], side_send.at[i, 2], side_recv.at[i, 2], across_y))
        ]
        diagonal[i][1].wait_recv()

        def act_high(k):
            held[i][k, y, 1 - x, :, half:] = held[i][k, y, 1 - x, :, half:] + high_half[i][k]

        each_row(act_high)
        block = held[i].at[:, y, 1 - x]
        side[i].append(
            launch(remote(block, from_x[i], side_send.at[i, 3], side_recv.at[i, 3], across_x))
        )

    def fold_side(i):
        for copy in side[i]:
            copy.wait_recv()

        def act(k):
            total = held[i][k, y, x].astype(jnp.float32) + from_x[i][k].astype(jnp.float32)
            held[i][k, y, x] = (total + from_y[i][k].astype(jnp.float32)).astype(jnp.bfloat16)

        each_row(act)
        last[i] = [
            launch(
                remote(
                    held[i].at[(z + k + 1) % depth, y, x],
                    from_row[i].at[k],
                    row_send.at[i, k],
                    row_recv.at[i, k],
                    device,
                )
            )
            for k, device in enumerate(row)
        ]

    def fold_row(i):
        for copy in last[i]:
            copy.wait_recv()
        total = held[i][z, y, x].astype(jnp.float32)
        for k in range(depth - 1):
            total = total + from_row[i][k].astype(jnp.float32)
        outs[i][...] = total

    for i in range(count):
        swap(i)
    for step in range(count + 3):
        for lag, act in enumerate((fold_core, fold_diagonal, fold_side, fold_row)):
            if 0 <= step - lag < count:
                act(step - lag)
    for copy in started:
        copy.wait_send()


def sum_shards(split, terms):
    count = len(terms)
    nz, ny, nx, _ = split
    blocks = [item.reshape(split + (-1, item.shape[-1])) for item in terms]
    shapes = [item.shape[4:] for item in blocks]
    low = jnp.bfloat16
    sem = pltpu.SemaphoreType.DMA
    scratch = [pltpu.VMEM((nz, ny, nx) + s, low) for s in shapes]
    scratch += [pltpu.VMEM((nz, s[0], s[1] // 2), low) for s in shapes] * 2
    scratch += [pltpu.VMEM((nz,) + s, low) for s in shapes] * 2
    scratch += [pltpu.VMEM((nz - 1,) + s, low) for s in shapes]
    scratch += [sem((count,))] * 2 + [sem((count, 4))] * 2 + [sem((count, nz - 1))] * 2
    return pl.pallas_call(
        functools.partial(sum_kernel, split, count),
        out_shape=[jax.ShapeDtypeStruct(s, jnp.float32) for s in shapes],
        in_specs=[pl.BlockSpec(memory_space=pltpu.VMEM)] * count,
        out_specs=[pl.BlockSpec(memory_space=pltpu.VMEM)] * count,
        scratch_shapes=scratch,
        compiler_params=pltpu.CompilerParams(
            collective_id=1, has_side_effects=True, vmem_limit_bytes=60 << 20
        ),
        name="sum_shards",
    )(*blocks)


def inner_split(rows):
    clips, frames = lax.axis_size("clip"), lax.axis_size("frame")
    if frames == 4 and clips % 2 == 0 and clips > 2 and rows % TILE_ROWS == 0:
        return (clips // 2, 2, 2, 2)
    return None


def pack_small(vectors, groups):
    rows = jnp.concatenate([item.reshape(groups, -1) for item in vectors], axis=1)
    size = SMALL_TILE[0] * SMALL_TILE[1]
    rows = jnp.pad(rows, ((0, 0), (0, size - rows.shape[1])))
    return rows.reshape((groups * SMALL_TILE[0], SMALL_TILE[1]))


def unpack_small(packed, widths):
    rows = packed.reshape(-1, SMALL_TILE[0] * SMALL_TILE[1])
    pieces, at = [], 0
    for width in widths:
        pieces.append(rows[:, at : at + width].reshape(-1))
        at += width
    return pieces


def gather_all(split, params):
    if split is None:
        return [lax.all_gather(item, ("clip", "frame"), axis=0, tiled=True) for item in params]
    wide = [k for k, item in enumerate(params) if item.ndim == 2]
    thin = [k for k, item in enumerate(params) if item.ndim == 1]
    full = gather_shards(split, [pack_small([params[k] for k in thin], 1)] + [params[k] for k in wide])
    vectors = unpack_small(full[0], [params[k].shape[0] for k in thin])
    result = dict(zip(wide, full[1:])) | dict(zip(thin, vectors))
    return [result[k] for k in range(len(params))]


def sum_all(split, terms):
    if split is None:
        groups = lax.axis_size("clip")
        received = [
            lax.all_to_all(
                item.astype(jnp.bfloat16), "clip", split_axis=0, concat_axis=0, tiled=True
            ).astype(jnp.float32)
            for item in stack_rows(terms, groups)
        ]
        return [
            lax.psum_scatter(
                item.astype(jnp.bfloat16), "frame", scatter_dimension=0, tiled=True
            ).astype(jnp.float32)
            for item in fold_rows(received)
        ]
    devices = split[0] * split[1] * split[2] * split[3]
    wide = [k for k, item in enumerate(terms) if item.ndim == 2]
    thin = [k for k, item in enumerate(terms) if item.ndim == 1]
    low = [item.astype(jnp.bfloat16) for item in terms]
    order = wide[::-1]
    sums = sum_shards(split, [low[k] for k in order] + [pack_small([low[k] for k in thin], devices)])
    vectors = unpack_small(sums[-1], [terms[k].shape[0] // devices for k in thin])
    result = dict(zip(order, sums[:-1])) | dict(zip(thin, vectors))
    return [result[k] for k in range(len(terms))]


VECTOR_ROWS = (0, 1, 10, 2, 3, 4, 5, 12, 6, 7, 8, 14, 9)


def on_device(
    video_tokens,
    time_gain,
    time_shift,
    time_inproj,
    time_inbias,
    time_outproj,
    time_outbias,
    time_linear,
    time_linbias,
    space_gain,
    space_shift,
    space_inproj,
    space_inbias,
    space_outproj,
    space_outbias,
    feed_gain,
    feed_shift,
    expand_weight,
    expand_bias,
    reduce_weight,
    reduce_bias,
    cotangent,
):
    split = inner_split(time_gain.shape[0])
    params = [
        time_gain,
        time_shift,
        time_inproj,
        time_inbias,
        time_outproj,
        time_outbias,
        time_linear,
        time_linbias,
        space_gain,
        space_shift,
        space_inproj,
        space_inbias,
        space_outproj,
        space_outbias,
        feed_gain,
        feed_shift,
        expand_weight,
        expand_bias,
        reduce_weight,
        reduce_bias,
    ]
    full = gather_all(split, params)
    frames, places, width = video_tokens.shape[1:]
    groups = lax.axis_size("frame")
    valid = places // groups
    block = -(-valid // TILE_ROWS) * TILE_ROWS
    rows = frames * groups * block

    def padded(tokens):
        cut = tokens.reshape((frames, groups, valid, width))
        return jnp.pad(cut, ((0, 0), (0, 0), (0, block - valid), (0, 0)))

    def to_places(tokens):
        return lax.all_to_all(
            tokens.reshape((frames, groups, block, width)),
            "frame",
            split_axis=1,
            concat_axis=0,
            tiled=True,
        ).reshape((rows, width))

    def to_frames(tokens):
        return lax.all_to_all(
            tokens.reshape((frames * groups, 1, block, width)),
            "frame",
            split_axis=0,
            concat_axis=1,
            tiled=True,
        ).reshape((rows, width))

    def trimmed(tokens):
        cut = tokens.reshape((frames, groups, block, width))[:, :, :valid]
        return cut.reshape((1, frames, places, width))

    def weight(item):
        return item.reshape((4, -1, item.shape[1]))

    thin = [item for item in full if item.ndim == 1]
    t_in, t_out, t_lin, s_in, s_out, w_up, w_down = [weight(item) for item in full if item.ndim == 2]
    pieces = sorted(zip(VECTOR_ROWS, thin), key=lambda pair: pair[0])
    vec = jnp.concatenate([item.reshape((-1, width)) for _, item in pieces], axis=0)
    vec = jnp.pad(vec, ((0, 24 - vec.shape[0]), (0, 0))).astype(WIDE)
    tokens, d_out = padded(video_tokens), padded(cotangent)
    own = tokens.reshape((rows, width))
    placed = to_places(tokens)
    b_t, a_t, z_t, p_t, o_t, u_t = time_forward(block, placed, vec, t_in, t_out, t_lin)
    layer_out, d_x1, d_b, g_s_in, g_s_out, g_up, g_down, sums_s = space_layer(
        (frames, valid, block),
        own,
        to_frames(b_t),
        d_out.reshape((rows, width)),
        vec,
        s_in,
        s_out,
        w_up,
        w_down,
    )
    d_t, g_t_in, g_t_out, g_t_lin, sums_t = time_backward(
        block, to_places(d_b), placed, a_t, z_t, p_t, o_t, u_t, vec, t_in, t_out, t_lin
    )
    input_grad = d_x1 + to_frames(d_t).astype(WIDE)
    sums = sums_s + sums_t
    wide = iter(
        [item.reshape((-1, width if item is g_down else item.shape[2])) for item in
         (g_t_in, g_t_out, g_t_lin, g_s_in, g_s_out, g_up, g_down)]
    )
    rows_of = iter(VECTOR_ROWS)
    terms = []
    for item in params:
        if item.ndim == 2:
            terms.append(next(wide))
        else:
            at = next(rows_of)
            count = item.shape[0] * lax.axis_size(("clip", "frame")) // width
            terms.append(sums[at : at + count].reshape(-1))
    summed = sum_all(split, terms)
    return (trimmed(layer_out), trimmed(input_grad)) + tuple(summed)


def solution(mesh):
    return jax.shard_map(
        on_device,
        mesh=mesh,
        in_specs=(
            P("clip", "frame", None, None),
            P(("clip", "frame")),
            P(("clip", "frame")),
            P(("clip", "frame"), None),
            P(("clip", "frame")),
            P(("clip", "frame"), None),
            P(("clip", "frame")),
            P(("clip", "frame"), None),
            P(("clip", "frame")),
            P(("clip", "frame")),
            P(("clip", "frame")),
            P(("clip", "frame"), None),
            P(("clip", "frame")),
            P(("clip", "frame"), None),
            P(("clip", "frame")),
            P(("clip", "frame")),
            P(("clip", "frame")),
            P(("clip", "frame"), None),
            P(("clip", "frame")),
            P(("clip", "frame"), None),
            P(("clip", "frame")),
            P("clip", "frame", None, None),
        ),
        out_specs=(
            P("clip", "frame", None, None),
            P("clip", "frame", None, None),
            P(("clip", "frame")),
            P(("clip", "frame")),
            P(("clip", "frame"), None),
            P(("clip", "frame")),
            P(("clip", "frame"), None),
            P(("clip", "frame")),
            P(("clip", "frame"), None),
            P(("clip", "frame")),
            P(("clip", "frame")),
            P(("clip", "frame")),
            P(("clip", "frame"), None),
            P(("clip", "frame")),
            P(("clip", "frame"), None),
            P(("clip", "frame")),
            P(("clip", "frame")),
            P(("clip", "frame")),
            P(("clip", "frame"), None),
            P(("clip", "frame")),
            P(("clip", "frame"), None),
            P(("clip", "frame")),
        ),
        check_vma=False,
    )
```

profile of v0, /device:TPU:0, one launch (start us, length us, event | category | flops | bytes accessed | tf_op | source)
XLA Modules:
  0.0 397.2 jit_solution(7742170533320903592)
XLA Ops:
  0.7 1.1 copy.59
  2.0 0.9 pad.19
  2.9 4.2 %all-to-all-start = ((bf16[2,4,56,768]{3,2,0,1:T(8,128)(2,1)}), bf16[2,4,56,768]{3,2,0,1:T(8,128)(2,1)S(1)}, u32[]{:S(2)}, u32[]{:S(2)}) async-start(bf16[2,4,56,768]{3,2,0,1:T(8,128)(2,1)} %pad.19), calls=%async_computation | async-start | bytes 1376256 | tf_op jit(solution)/shard_map/all_to_all | solution.py:903
  7.9 100.2 %gather_shards.1 = (bf16[4,2,2,2,8,256]{5,4,3,2,1,0:T(8,128)(2,1)}, bf16[4,2,2,2,24,2304]{5,4,3,2,1,0:T(8,128)(2,1)}, bf16[4,2,2,2,24,768]{5,4,3,2,1,0:T(8,128)(...) custom-call(bf16[8,256]{1,0:T(8,128)(2,1)} %reshape.247.refs_0_, ...), custom_call_target="tpu_custom_call" | custom-call | tf_op jit(solution)/shard_map/gather_shards/pallas_call | solution.py:635
  108.2 0.9 copy.69
  111.5 0.9 copy-done
  112.4 18.2 %time_forward.1 = (bf16[448,768]{1,0:T(8,128)(2,1)}, bf16[448,768]{1,0:T(8,128)(2,1)}, bf16[448,2304]{1,0:T(8,128)(2,1)}, f32[8,448,128]{2,1,0:T(8,128)}, bf16[4...) custom-call(bf16[448,768]{1,0:T(8,128)(2,1)} %bitcast.101, f32[24,768]{1,0:T(8,128)} %pad_convert_fusion.vec_ref, ...), custom_call_target="tpu_custom_call" | custom-call | tf_op jit(solution)/shard_map/time_forward/pallas_call | solution.py:384
  130.5 4.4 %all-to-all-start.1 = ((bf16[8,1,56,768]{3,2,1,0:T(8,128)(2,1)}), bf16[8,1,56,768]{3,2,1,0:T(8,128)(2,1)S(1)}, u32[]{:S(2)}, u32[]{:S(2)}) async-start(bf16[8,1,56,768]{3,2,1,0:T(8,128)(2,1)} %bitcast.128), calls=%async_computation.1 | async-start | bytes 1376256 | tf_op jit(solution)/shard_map/all_to_all | solution.py:912
  135.0 2.0 copy.60
  137.0 0.9 pad.22
  138.0 8.2 %all-to-all-done.1 = bf16[8,1,56,768]{3,2,1,0:T(8,128)(2,1)S(1)} async-done(((bf16[8,1,56,768]{3,2,1,0:T(8,128)(2,1)}), bf16[8,1,56,768]{3,2,1,0:T(8,128)(2,1)S(1)}, u32[]{:S(2)}, u32[]{:S(2)}) %all-to-all-start.1) | async-done | bytes 688160 | tf_op jit(solution)/shard_map/all_to_all | solution.py:912
  146.2 0.9 copy.62
  147.1 75.6 %space_layer.1 = (bf16[448,768]{1,0:T(8,128)(2,1)}, f32[448,768]{1,0:T(8,128)}, bf16[448,768]{1,0:T(8,128)(2,1)}, bf16[4,192,2304]{2,1,0:T(8,128)(2,1)}, bf16[4,...) custom-call(bf16[448,768]{1,0:T(8,128)(2,1)} %bitcast.115, ...), custom_call_target="tpu_custom_call" | custom-call | tf_op jit(solution)/shard_map/space_layer/pallas_call | solution.py:384
  222.7 2.1 copy.65
  224.8 3.7 all-to-all-start.2
  228.5 1.4 copy.64
  229.9 8.9 %all-to-all-done.2 = bf16[2,4,56,768]{3,2,0,1:T(8,128)(2,1)S(1)} async-done(((bf16[2,4,56,768]{3,2,0,1:T(8,128)(2,1)}), bf16[2,4,56,768]{3,2,0,1:T(8,128)(2,1)S(1)}, u32[]{:S(2)}, u32[]{:S(2)}) %all-to-all-start.2) | async-done | bytes 688160 | tf_op jit(solution)/shard_map/all_to_all | solution.py:903
  238.8 0.9 copy-done.1
  239.7 28.0 %time_backward.1 = (bf16[448,768]{1,0:T(8,128)(2,1)}, bf16[4,192,2304]{2,1,0:T(8,128)(2,1)}, bf16[4,192,768]{2,1,0:T(8,128)(2,1)}, bf16[4,192,768]{2,1,0:T(8,128)(2,1)}, f32[24,768]{1,0:T(8,128)}) custom-call(bf16[448,768]{1,0:T(8,128)(2,1)} %bitcast.120, bf16[448,768]{1,0:T(8,128)(2,1)} %bitcast.102, bf16[448,768]{1,0:T(8,128)(2,1)} %get-tuple-element.69.a_ref, ...), custom_call_target="tpu_custom_call" | custom-call | tf_op jit(solution)/shard_map/time_backward/pallas_call | solution.py:384
  267.7 0.9 add_convert_fusion
  270.0 3.5 all-to-all-start.3
  274.3 113.2 %sum_shards.1 = (f32[96,768]{1,0:T(8,128)}, f32[24,3072]{1,0:T(8,128)}, f32[24,768]{1,0:T(8,128)}, f32[24,2304]{1,0:T(8,128)}, f32[24,768]{1,0:T(8,128)}, /*inde...) custom-call(bf16[4,2,2,2,96,768]{5,4,3,2,1,0:T(8,128)(2,1)} %bitcast.109, ...), custom_call_target="tpu_custom_call" | custom-call | tf_op jit(solution)/shard_map/sum_shards/pallas_call | solution.py:768
  387.5 0.8 copy.71
  390.5 2.0 copy.68
  (105 shorter events, 12.1 us)
Async XLA Ops:
  1.8 5.3 %copy-start.13 = (bf16[24]{0:T(256)(128)(2,1)S(1)}, bf16[24]{0:T(256)(128)(2,1)}, u32[]{:S(2)}) copy-start(bf16[24]{0:T(256)(128)(2,1)} %param.23) | copy-start | bytes 148
  1.8 5.3 %copy-start.14 = (bf16[24]{0:T(256)(128)(2,1)S(1)}, bf16[24]{0:T(256)(128)(2,1)}, u32[]{:S(2)}) copy-start(bf16[24]{0:T(256)(128)(2,1)} %param.24) | copy-start | bytes 148
  1.8 5.2 %copy-start.15 = (bf16[48]{0:T(256)(128)(2,1)S(1)}, bf16[48]{0:T(256)(128)(2,1)}, u32[]{:S(2)}) copy-start(bf16[48]{0:T(256)(128)(2,1)} %param.26) | copy-start | bytes 292
  1.8 5.2 %copy-start.16 = (bf16[24]{0:T(256)(128)(2,1)S(1)}, bf16[24]{0:T(256)(128)(2,1)}, u32[]{:S(2)}) copy-start(bf16[24]{0:T(256)(128)(2,1)} %param.28) | copy-start | bytes 148
  1.9 5.2 %copy-start.17 = (bf16[24]{0:T(256)(128)(2,1)S(1)}, bf16[24]{0:T(256)(128)(2,1)}, u32[]{:S(2)}) copy-start(bf16[24]{0:T(256)(128)(2,1)} %param.30) | copy-start | bytes 148
  1.9 5.2 %copy-start.18 = (bf16[24]{0:T(256)(128)(2,1)S(1)}, bf16[24]{0:T(256)(128)(2,1)}, u32[]{:S(2)}) copy-start(bf16[24]{0:T(256)(128)(2,1)} %param.31) | copy-start | bytes 148
  1.9 5.2 %copy-start.19 = (bf16[24]{0:T(256)(128)(2,1)S(1)}, bf16[24]{0:T(256)(128)(2,1)}, u32[]{:S(2)}) copy-start(bf16[24]{0:T(256)(128)(2,1)} %param.32) | copy-start | bytes 148
  1.9 5.2 %copy-start.20 = (bf16[48]{0:T(256)(128)(2,1)S(1)}, bf16[48]{0:T(256)(128)(2,1)}, u32[]{:S(2)}) copy-start(bf16[48]{0:T(256)(128)(2,1)} %param.34) | copy-start | bytes 292
  1.9 5.2 %copy-start.21 = (bf16[24]{0:T(256)(128)(2,1)S(1)}, bf16[24]{0:T(256)(128)(2,1)}, u32[]{:S(2)}) copy-start(bf16[24]{0:T(256)(128)(2,1)} %param.36) | copy-start | bytes 148
  1.9 5.2 %copy-start.22 = (bf16[24]{0:T(256)(128)(2,1)S(1)}, bf16[24]{0:T(256)(128)(2,1)}, u32[]{:S(2)}) copy-start(bf16[24]{0:T(256)(128)(2,1)} %param.37) | copy-start | bytes 148
  1.9 5.2 %copy-start.23 = (bf16[24]{0:T(256)(128)(2,1)S(1)}, bf16[24]{0:T(256)(128)(2,1)}, u32[]{:S(2)}) copy-start(bf16[24]{0:T(256)(128)(2,1)} %param.38) | copy-start | bytes 148
  1.9 5.2 %copy-start.24 = (bf16[96]{0:T(256)(128)(2,1)S(1)}, bf16[96]{0:T(256)(128)(2,1)}, u32[]{:S(2)}) copy-start(bf16[96]{0:T(256)(128)(2,1)} %param.40) | copy-start | bytes 580
  1.9 5.2 %copy-start.25 = (bf16[24]{0:T(256)(128)(2,1)S(1)}, bf16[24]{0:T(256)(128)(2,1)}, u32[]{:S(2)}) copy-start(bf16[24]{0:T(256)(128)(2,1)} %param.42) | copy-start | bytes 148
  2.9 108.6 %all-to-all-start = ((bf16[2,4,56,768]{3,2,0,1:T(8,128)(2,1)}), bf16[2,4,56,768]{3,2,0,1:T(8,128)(2,1)S(1)}, u32[]{:S(2)}, u32[]{:S(2)}) async-start(bf16[2,4,56,768]{3,2,0,1:T(8,128)(2,1)} %pad.19), calls=%async_computation | async-start | bytes 1376256 | tf_op jit(solution)/shard_map/all_to_all | solution.py:903
  130.5 6.4 %copy-start.4 = (bf16[1,2,196,768]{3,1,2,0:T(2,128)(2,1)S(1)}, bf16[1,2,196,768]{3,1,2,0:T(2,128)(2,1)}, u32[]{:S(2)}) copy-start(bf16[1,2,196,768]{3,1,2,0:T(2,128)(2,1)} %param.43) | copy-start | bytes 1806340
  130.5 15.6 %all-to-all-start.1 = ((bf16[8,1,56,768]{3,2,1,0:T(8,128)(2,1)}), bf16[8,1,56,768]{3,2,1,0:T(8,128)(2,1)S(1)}, u32[]{:S(2)}, u32[]{:S(2)}) async-start(bf16[8,1,56,768]{3,2,1,0:T(8,128)(2,1)} %bitcast.128), calls=%async_computation.1 | async-start | bytes 1376256 | tf_op jit(solution)/shard_map/all_to_all | solution.py:912
  222.7 5.8 %copy-start.3 = (bf16[448,768]{1,0:T(8,128)(2,1)S(1)}, bf16[448,768]{1,0:T(8,128)(2,1)}, u32[]{:S(2)}) copy-start(bf16[448,768]{1,0:T(8,128)(2,1)} %get-tuple-element.66) | copy-start | bytes 2064388
  224.8 14.1 %all-to-all-start.2 = ((bf16[2,4,56,768]{3,2,0,1:T(8,128)(2,1)}), bf16[2,4,56,768]{3,2,0,1:T(8,128)(2,1)S(1)}, u32[]{:S(2)}, u32[]{:S(2)}) async-start(bf16[2,4,56,768]{3,2,0,1:T(8,128)(2,1)} %copy.65), calls=%async_computation.2 | async-start | bytes 1376256 | tf_op jit(solution)/shard_map/all_to_all | solution.py:903
  239.7 28.0 %copy-start.12 = (f32[24,768]{1,0:T(8,128)S(1)}, f32[24,768]{1,0:T(8,128)}, u32[]{:S(2)}) copy-start(f32[24,768]{1,0:T(8,128)} %get-tuple-element.82) | copy-start | bytes 221188
  270.0 120.2 %all-to-all-start.3 = ((bf16[8,1,56,768]{3,2,1,0:T(8,128)(2,1)}), bf16[8,1,56,768]{3,2,1,0:T(8,128)(2,1)S(1)}, u32[]{:S(2)}, u32[]{:S(2)}) async-start(bf16[8,1,56,768]{3,2,1,0:T(8,128)(2,1)} %bitcast.126), calls=%async_computation.3 | async-start | bytes 1376256 | tf_op jit(solution)/shard_map/all_to_all | solution.py:912
  390.5 3.9 copy-start.7
  390.5 4.6 %copy-start.9 = (f32[24,768]{1,0:T(8,128)S(1)}, f32[24,768]{1,0:T(8,128)}, u32[]{:S(2)}) copy-start(f32[24,768]{1,0:T(8,128)} %get-tuple-element.164) | copy-start | bytes 221188
  390.5 5.2 %copy-start.6 = (f32[24,3072]{1,0:T(8,128)S(1)}, f32[24,3072]{1,0:T(8,128)}, u32[]{:S(2)}) copy-start(f32[24,3072]{1,0:T(8,128)} %get-tuple-element.168) | copy-start | bytes 884740
  392.5 4.0 %copy-start.5 = (f32[96,768]{1,0:T(8,128)S(1)}, f32[96,768]{1,0:T(8,128)}, u32[]{:S(2)}) copy-start(f32[96,768]{1,0:T(8,128)} %get-tuple-element.170) | copy-start | bytes 884740
  (6 other events, 12.5 us)
where the time goes:
time: 398 us; the launch traced here: 397 us
  Pallas kernels  335 us (84%)
  local copies, waits for them, and re-layouts  26.1 us (7%)
  waiting for transfers between devices  17.1 us (4%)
  starting transfers between devices  15.8 us (4%)
    pallas_call x3, Pallas kernels, vmem_call(): pl.pallas_call(body, out_shape=[jax.ShapeDtypeStruct(shape, kind) for sha...  122 us
    pallas_call x1, Pallas kernels, sum_shards(): pl.pallas_call(functools.partial(sum_kernel, split, count), out_shape=[ja...  113 us
    pallas_call x1, Pallas kernels, gather_shards(): pl.pallas_call(functools.partial(gather_kernel, split, count), out_shape=...  100 us
    unnamed x62, local copies, waits for them, and re-layouts  9.01 us
    all_to_all x2, waiting for transfers between devices, to_places(): lax.all_to_all(tokens.reshape((frames, groups, block, width)), 'frame', s...  8.89 us
    all_to_all x2, waiting for transfers between devices, to_frames(): lax.all_to_all(tokens.reshape((frames * groups, 1, block, width)), 'frame...  8.18 us
  transfers between devices with their start and end apart: 4, of which 2 were waited for; matrix products, arithmetic and copies ran while one was open for 3% of the time, Pallas kernels for 54%

commit v1 on v0

--- a/solution.py
+++ b/solution.py
@@ -7,6 +7,8 @@
 from jax.experimental.pallas import tpu as pltpu
 from jax.sharding import PartitionSpec as P
 
+MESH = pl.DeviceIdType.MESH
+TILE_ROWS = 8
 LOW = jnp.bfloat16
 WIDE = jnp.float32
 HEADS = 12
@@ -24,12 +26,12 @@
     return lax.dot_general(a, b, (((1,), (1,)), ((), ())), preferred_element_type=WIDE)
 
 
-def each(count, act):
+def each(count, act, start=0):
     def step(k, carry):
         act(k)
         return carry
 
-    lax.fori_loop(0, count, step, 0)
+    lax.fori_loop(start, count, step, 0)
 
 
 def tiles(k, size=TILE):
@@ -39,6 +41,22 @@
 def columns(w_ref, cut):
     block = w_ref[:, :, cut]
     return block.reshape((block.shape[0] * block.shape[1], block.shape[2]))
+
+
+def wide_rows(ref, k, size):
+    if len(ref.shape) == 2:
+        return ref[tiles(k, size), :].astype(WIDE)
+    per = size // ref.shape[1]
+    block = ref[pl.ds(k * per, per), :, :].astype(WIDE)
+    return block.reshape((size, ref.shape[2]))
+
+
+def put_rows(ref, k, size, value):
+    if len(ref.shape) == 2:
+        ref[tiles(k, size), :] = value.astype(ref.dtype)
+    else:
+        per = size // ref.shape[1]
+        ref[pl.ds(k * per, per), :, :] = value.reshape((per,) + ref.shape[1:]).astype(ref.dtype)
 
 
 def normal(x):
@@ -51,34 +69,32 @@
     gain, shift = vec[gain_row : gain_row + 1, :], vec[gain_row + 1 : gain_row + 2, :]
 
     def act(k):
-        rows = tiles(k, block)
-        unit, _ = normal(x_ref[rows, :].astype(WIDE))
-        a_ref[rows, :] = (unit * gain + shift).astype(LOW)
-
-    each(x_ref.shape[0] // block, act)
+        unit, _ = normal(wide_rows(x_ref, k, block))
+        a_ref[tiles(k, block), :] = (unit * gain + shift).astype(LOW)
+
+    each(a_ref.shape[0] // block, act)
 
 
 def norm_back_stage(x_ref, vec, gain_row, da_ref, sums, block, store):
     gain = vec[gain_row : gain_row + 1, :]
-    width = x_ref.shape[1]
+    width = da_ref.shape[1]
 
     def step(k, carry):
-        rows = tiles(k, block)
-        unit, inverse = normal(x_ref[rows, :].astype(WIDE))
-        da = da_ref[rows, :]
+        unit, inverse = normal(wide_rows(x_ref, k, block))
+        da = da_ref[tiles(k, block), :]
         e = da * gain
         dv = inverse * (
             e
             - jnp.mean(e, axis=-1, keepdims=True)
             - unit * jnp.mean(e * unit, axis=-1, keepdims=True)
         )
-        store(rows, dv)
+        store(k, dv)
         grad_gain, grad_shift = carry
         fold = lambda v: jnp.sum(v.reshape(block // 8, 8, width), axis=0)
         return grad_gain + fold(da * unit), grad_shift + fold(da)
 
     zero = jnp.zeros((8, width), WIDE)
-    grad_gain, grad_shift = lax.fori_loop(0, x_ref.shape[0] // block, step, (zero, zero))
+    grad_gain, grad_shift = lax.fori_loop(0, da_ref.shape[0] // block, step, (zero, zero))
     sums[gain_row : gain_row + 1, :] = jnp.sum(grad_gain, axis=0, keepdims=True)
     sums[gain_row + 1 : gain_row + 2, :] = jnp.sum(grad_shift, axis=0, keepdims=True)
 
@@ -162,7 +178,7 @@
     return lane < LANES // 2
 
 
-def space_attend(z_ref, p_ref, o_ref, frames, rows, valid, block):
+def space_attend(z_ref, p_ref, o_ref, frames, rows, valid, block, start=0, stop=None):
     width = o_ref.shape[1]
     pairs = width // LANES
     scale = (LANES // 2) ** -0.5
@@ -189,10 +205,10 @@
         o = jnp.where(top, outs[0], outs[1]).T
         o_ref[span, pl.ds(pl.multiple_of(pair * LANES, LANES), LANES)] = o.astype(LOW)
 
-    each(frames * pairs, act)
-
-
-def space_attend_back(z_ref, p_ref, do_ref, dz_ref, frames, rows):
+    each(frames * pairs if stop is None else stop, act, start)
+
+
+def space_attend_back(z_ref, p_ref, do_ref, dz_ref, frames, rows, start=0, stop=None):
     width = do_ref.shape[1]
     pairs = width // LANES
     scale = (LANES // 2) ** -0.5
@@ -227,7 +243,7 @@
         dz_ref[span, cut_k] = (dk * scale).astype(LOW)
         dz_ref[span, cut_v] = dv.astype(LOW)
 
-    each(frames * pairs, act)
+    each(frames * pairs if stop is None else stop, act, start)
 
 
 def head_sum(width):
@@ -248,7 +264,7 @@
     return dot(high, pick) + dot(rest, pick)
 
 
-def time_attend(z_ref, p_ref, o_ref, frames, block):
+def time_attend(z_ref, p_ref, o_ref, frames, block, start=0, stop=None):
     width = o_ref.shape[1]
     scale = (width // HEADS) ** -0.5
     pick, spread = head_sum(width), head_spread(width)
@@ -273,14 +289,15 @@
             v = z_ref[span, 2 * width :].astype(WIDE)
             for half in range(2):
                 p = probs[half][k]
+                p = p.astype(LOW)
                 p_ref[2 * pair + half, span, :] = p
-                out[half] = out[half] + dot(p.astype(LOW), spread) * v
+                out[half] = out[half] + dot(p, spread) * v
         o_ref[rows, :] = jnp.concatenate(out, axis=0).astype(LOW)
 
-    each(frames // 2, act)
-
-
-def time_attend_back(z_ref, p_ref, do_ref, dz_ref, dk_ref, dv_ref, frames, block):
+    each(frames // 2 if stop is None else stop, act, start)
+
+
+def time_attend_back(z_ref, p_ref, do_ref, dz_ref, dk_ref, dv_ref, frames, block, between=None):
     width = do_ref.shape[1]
     scale = (width // HEADS) ** -0.5
     pick, spread = head_sum(width), head_spread(width)
@@ -298,7 +315,7 @@
             v = z_ref[span, 2 * width :].astype(WIDE)
             for half in range(2):
                 dp = by_head(do[spans[half]] * v, pick)
-                inner[half] = inner[half] + dp * p_ref[2 * pair + half, span, :]
+                inner[half] = inner[half] + dp * p_ref[2 * pair + half, span, :].astype(WIDE)
                 dps[half].append(dp)
         dq = [jnp.zeros((block, width), WIDE)] * 2
         for at, span in enumerate(spans):
@@ -306,15 +323,21 @@
             dk, dv = dk_ref[span, :], dv_ref[span, :]
             for half in range(2):
                 p = p_ref[2 * pair + half, span, :]
-                ds = dot((p * (dps[half][at] - inner[half])).astype(LOW), spread)
+                ds = dot((p.astype(WIDE) * (dps[half][at] - inner[half])).astype(LOW), spread)
                 dq[half] = dq[half] + ds * k
                 dk = dk + ds * q[spans[half]]
-                dv = dv + dot(p.astype(LOW), spread) * do[spans[half]]
+                dv = dv + dot(p, spread) * do[spans[half]]
             dk_ref[span, :] = dk
             dv_ref[span, :] = dv
         dz_ref[rows, :width] = (jnp.concatenate(dq, axis=0) * scale).astype(LOW)
 
-    each(frames // 2, act)
+    if between is None:
+        each(frames // 2, act)
+    else:
+        each(frames // 4, act)
+        between()
+        each(frames // 2, act, frames // 4)
+        between()
 
     def out(pair):
         rows = tiles(pair, 2 * block)
@@ -324,7 +347,7 @@
     each(frames // 2, out)
 
 
-def expand_stage(a_ref, w_ref, vec, g_ref, slope_ref):
+def expand_stage(a_ref, w_ref, vec, g_ref, slope_ref, start=0, stop=None):
     width = a_ref.shape[1]
     per = width // TILE
 
@@ -338,7 +361,7 @@
         g_ref[:, cut] = (h * cdf).astype(LOW)
         slope_ref[:, cut] = (cdf + h * (jnp.exp(-0.5 * h * h) * 0.3989422804014327)).astype(LOW)
 
-    each(w_ref.shape[2] // TILE, act)
+    each(w_ref.shape[2] // TILE if stop is None else stop, act, start)
 
 
 def reduce_stage(g_ref, w_ref, vec, x_ref, out_store):
@@ -410,7 +433,7 @@
         project_stage(u_ref, w_lin, vec_ref, T_LINB, store(b_ref))
 
     token = ((rows, width), LOW)
-    outs = [token, token, ((rows, 3 * width), LOW), ((frames, rows, LANES), WIDE), token, token]
+    outs = [token, token, ((rows, 3 * width), LOW), ((frames, rows, LANES), LOW), token, token]
     return vmem_call(body, outs, (x, vec, w_in, w_out, w_lin), [], "time_forward")
 
 
@@ -451,7 +474,8 @@
         weight_stage(at, dh, g_up, bias_rows(sums, [E_BIAS + k for k in range(hidden // width)], width))
         back_stage(dh, w_up, acc)
 
-        def put_x2(r, dv):
+        def put_x2(k, dv):
+            r = tiles(k, 2 * block)
             total = dy_ref[r, :].astype(WIDE) + dv
             dx1_ref[r, :] = total
             low[r, :] = total.astype(LOW)
@@ -467,7 +491,8 @@
         weight_stage(at, dz, g_in, bias_rows(sums, [S_INB, None, S_INB + 1], width))
         back_stage(dz, w_in, acc)
 
-        def put_x1(r, dv):
+        def put_x1(k, dv):
+            r = tiles(k, 2 * block)
             total = dx1_ref[r, :] + dv
             dx1_ref[r, :] = total
             db_ref[r, :] = total.astype(LOW)
@@ -501,8 +526,8 @@
         weight_stage(at, dz, g_in, bias_rows(sums, [T_INB, None, T_INB + 1], width))
         back_stage(dz, w_in, acc)
 
-        def put(r, dv):
-            dt_ref[r, :] = dv.astype(LOW)
+        def put(k, dv):
+            put_rows(dt_ref, k, 2 * block, dv)
 
         norm_back_stage(x_ref, vec_ref, T_GAIN, acc, sums, 2 * block, put)
 
@@ -520,11 +545,6 @@
 
 def fold_rows(received):
     return tuple((jnp.sum(item, axis=0) for item in received))
-
-
-MESH = pl.DeviceIdType.MESH
-TILE_ROWS = 8
-SMALL_TILE = (8, 256)
 
 
 def remote(source, target, send, recv, device):
@@ -558,226 +578,6 @@
     pl.semaphore_wait(barrier, len(devices))
 
 
-def gather_kernel(split, count, *refs):
-    shards, full = refs[:count], refs[count : 2 * count]
-    row_send, row_recv, side_send, side_recv, core_send, core_recv, own_sem = refs[2 * count :]
-    (z, y, x, c), row, (across_x, across_y, twin) = place(split)
-    greet(row + [across_x, across_y, twin])
-    started, first, second, third, core = [], {}, {}, {}, {}
-
-    def launch(copy):
-        copy.start()
-        started.append(copy)
-        return copy
-
-    def to_twin(i, step, block):
-        return launch(remote(block, block, core_send.at[i, step], core_recv.at[i, step], twin))
-
-    def spread(i):
-        own = full[i].at[z, y, x, c]
-        first[i] = [
-            launch(remote(shards[i], own, row_send.at[i, k], row_recv.at[i, k], device))
-            for k, device in enumerate(row)
-        ]
-        keep = pltpu.make_async_copy(shards[i], own, own_sem.at[i])
-        keep.start()
-        first[i].append(keep)
-
-    def sideways(i):
-        for copy in first[i][:-1]:
-            copy.wait_recv()
-        first[i][-1].wait()
-        block = full[i].at[:, y, x, c]
-        second[i] = [
-            launch(remote(block, block, side_send.at[i, k], side_recv.at[i, k], device))
-            for k, device in enumerate((across_x, across_y))
-        ]
-        core[i] = [to_twin(i, 0, block)]
-
-    def relay(i):
-        half = shards[i].shape[-1] // 2
-        second[i][0].wait_recv()
-        part = full[i].at[:, y, 1 - x, c, :, pl.ds(0, half)]
-        third[i] = [launch(remote(part, part, side_send.at[i, 2], side_recv.at[i, 2], across_y))]
-        core[i].append(to_twin(i, 1, full[i].at[:, y, 1 - x, c]))
-        second[i][1].wait_recv()
-        part = full[i].at[:, 1 - y, x, c, :, pl.ds(half, half)]
-        third[i].append(
-            launch(remote(part, part, side_send.at[i, 3], side_recv.at[i, 3], across_x))
-        )
-        core[i].append(to_twin(i, 2, full[i].at[:, 1 - y, x, c]))
-
-    def finish(i):
-        for copy in third[i]:
-            copy.wait_recv()
-        core[i].append(to_twin(i, 3, full[i].at[:, 1 - y, 1 - x, c]))
-
-    def receive(i):
-        for copy in core[i]:
-            copy.wait_recv()
-
-    ahead = 2
-    for i in range(min(ahead, count)):
-        spread(i)
-    for step in range(count + 3):
-        for lag, act in enumerate((sideways, relay, finish, receive)):
-            if 0 <= step - lag < count:
-                act(step - lag)
-            if lag == 0 and step + ahead < count:
-                spread(step + ahead)
-    for copy in started:
-        copy.wait_send()
-
-
-def gather_shards(split, shards):
-    count = len(shards)
-    sem = pltpu.SemaphoreType.DMA
-    full = pl.pallas_call(
-        functools.partial(gather_kernel, split, count),
-        out_shape=[jax.ShapeDtypeStruct(split + item.shape, item.dtype) for item in shards],
-        in_specs=[pl.BlockSpec(memory_space=pl.ANY)] * count,
-        out_specs=[pl.BlockSpec(memory_space=pl.ANY)] * count,
-        scratch_shapes=[sem((count, split[0] - 1))] * 2 + [sem((count, 4))] * 4 + [sem((count,))],
-        compiler_params=pltpu.CompilerParams(collective_id=0, has_side_effects=True),
-        name="gather_shards",
-    )(*shards)
-    return [item.reshape((-1, item.shape[-1])) for item in full]
-
-
-def sum_kernel(split, count, *refs):
-    groups = [refs[k * count : (k + 1) * count] for k in range(8)]
-    mine, outs, held, low_half, high_half, from_x, from_y, from_row = groups
-    core_send, core_recv, side_send, side_recv, row_send, row_recv = refs[8 * count :]
-    (z, y, x, c), row, (across_x, across_y, twin) = place(split)
-    greet(row + [across_x, across_y, twin])
-    depth = split[0]
-    started, core, diagonal, side, last = [], {}, {}, {}, {}
-
-    def launch(copy):
-        copy.start()
-        started.append(copy)
-        return copy
-
-    def each_row(act):
-        def step(k, carry):
-            act(k)
-            return carry
-
-        lax.fori_loop(0, depth, step, 0)
-
-    def swap(i):
-        block = mine[i].at[:, :, :, 1 - c]
-        core[i] = launch(remote(block, held[i], core_send.at[i], core_recv.at[i], twin))
-
-    def fold_core(i):
-        core[i].wait_recv()
-        half = mine[i].shape[-1] // 2
-
-        def fold(yy, xx):
-            def act(k):
-                held[i][k, yy, xx] = held[i][k, yy, xx] + mine[i][k, yy, xx, c]
-
-            each_row(act)
-
-        fold(1 - y, 1 - x)
-        low = held[i].at[:, 1 - y, 1 - x, :, pl.ds(0, half)]
-        high = held[i].at[:, 1 - y, 1 - x, :, pl.ds(half, half)]
-        diagonal[i] = [
-            launch(remote(low, low_half[i], side_send.at[i, 0], side_recv.at[i, 0], across_x)),
-            launch(remote(high, high_half[i], side_send.at[i, 1], side_recv.at[i, 1], across_y)),
-        ]
-        fold(1 - y, x)
-        fold(y, 1 - x)
-        fold(y, x)
-
-    def fold_diagonal(i):
-        half = mine[i].shape[-1] // 2
-        diagonal[i][0].wait_recv()
-
-        def act_low(k):
-            held[i][k, 1 - y, x, :, :half] = held[i][k, 1 - y, x, :, :half] + low_half[i][k]
-
-        each_row(act_low)
-        block = held[i].at[:, 1 - y, x]
-        side[i] = [
-            launch(remote(block, from_y[i], side_send.at[i, 2], side_recv.at[i, 2], across_y))
-        ]
-        diagonal[i][1].wait_recv()
-
-        def act_high(k):
-            held[i][k, y, 1 - x, :, half:] = held[i][k, y, 1 - x, :, half:] + high_half[i][k]
-
-        each_row(act_high)
-        block = held[i].at[:, y, 1 - x]
-        side[i].append(
-            launch(remote(block, from_x[i], side_send.at[i, 3], side_recv.at[i, 3], across_x))
-        )
-
-    def fold_side(i):
-        for copy in side[i]:
-            copy.wait_recv()
-
-        def act(k):
-            total = held[i][k, y, x].astype(jnp.float32) + from_x[i][k].astype(jnp.float32)
-            held[i][k, y, x] = (total + from_y[i][k].astype(jnp.float32)).astype(jnp.bfloat16)
-
-        each_row(act)
-        last[i] = [
-            launch(
-                remote(
-                    held[i].at[(z + k + 1) % depth, y, x],
-                    from_row[i].at[k],
-                    row_send.at[i, k],
-                    row_recv.at[i, k],
-                    device,
-                )
-            )
-            for k, device in enumerate(row)
-        ]
-
-    def fold_row(i):
-        for copy in last[i]:
-            copy.wait_recv()
-        total = held[i][z, y, x].astype(jnp.float32)
-        for k in range(depth - 1):
-            total = total + from_row[i][k].astype(jnp.float32)
-        outs[i][...] = total
-
-    for i in range(count):
-        swap(i)
-    for step in range(count + 3):
-        for lag, act in enumerate((fold_core, fold_diagonal, fold_side, fold_row)):
-            if 0 <= step - lag < count:
-                act(step - lag)
-    for copy in started:
-        copy.wait_send()
-
-
-def sum_shards(split, terms):
-    count = len(terms)
-    nz, ny, nx, _ = split
-    blocks = [item.reshape(split + (-1, item.shape[-1])) for item in terms]
-    shapes = [item.shape[4:] for item in blocks]
-    low = jnp.bfloat16
-    sem = pltpu.SemaphoreType.DMA
-    scratch = [pltpu.VMEM((nz, ny, nx) + s, low) for s in shapes]
-    scratch += [pltpu.VMEM((nz, s[0], s[1] // 2), low) for s in shapes] * 2
-    scratch += [pltpu.VMEM((nz,) + s, low) for s in shapes] * 2
-    scratch += [pltpu.VMEM((nz - 1,) + s, low) for s in shapes]
-    scratch += [sem((count,))] * 2 + [sem((count, 4))] * 2 + [sem((count, nz - 1))] * 2
-    return pl.pallas_call(
-        functools.partial(sum_kernel, split, count),
-        out_shape=[jax.ShapeDtypeStruct(s, jnp.float32) for s in shapes],
-        in_specs=[pl.BlockSpec(memory_space=pltpu.VMEM)] * count,
-        out_specs=[pl.BlockSpec(memory_space=pltpu.VMEM)] * count,
-        scratch_shapes=scratch,
-        compiler_params=pltpu.CompilerParams(
-            collective_id=1, has_side_effects=True, vmem_limit_bytes=60 << 20
-        ),
-        name="sum_shards",
-    )(*blocks)
-
-
 def inner_split(rows):
     clips, frames = lax.axis_size("clip"), lax.axis_size("frame")
     if frames == 4 and clips % 2 == 0 and clips > 2 and rows % TILE_ROWS == 0:
@@ -785,60 +585,683 @@
     return None
 
 
-def pack_small(vectors, groups):
-    rows = jnp.concatenate([item.reshape(groups, -1) for item in vectors], axis=1)
-    size = SMALL_TILE[0] * SMALL_TILE[1]
-    rows = jnp.pad(rows, ((0, 0), (0, size - rows.shape[1])))
-    return rows.reshape((groups * SMALL_TILE[0], SMALL_TILE[1]))
-
-
-def unpack_small(packed, widths):
-    rows = packed.reshape(-1, SMALL_TILE[0] * SMALL_TILE[1])
-    pieces, at = [], 0
-    for width in widths:
-        pieces.append(rows[:, at : at + width].reshape(-1))
-        at += width
-    return pieces
-
-
-def gather_all(split, params):
-    if split is None:
-        return [lax.all_gather(item, ("clip", "frame"), axis=0, tiled=True) for item in params]
-    wide = [k for k, item in enumerate(params) if item.ndim == 2]
-    thin = [k for k, item in enumerate(params) if item.ndim == 1]
-    full = gather_shards(split, [pack_small([params[k] for k in thin], 1)] + [params[k] for k in wide])
-    vectors = unpack_small(full[0], [params[k].shape[0] for k in thin])
-    result = dict(zip(wide, full[1:])) | dict(zip(thin, vectors))
-    return [result[k] for k in range(len(params))]
-
-
-def sum_all(split, terms):
-    if split is None:
-        groups = lax.axis_size("clip")
-        received = [
-            lax.all_to_all(
-                item.astype(jnp.bfloat16), "clip", split_axis=0, concat_axis=0, tiled=True
-            ).astype(jnp.float32)
-            for item in stack_rows(terms, groups)
+SMALL_ROWS = 16
+RING = 6
+STAGES = 3
+SUB = 4
+
+
+class Gather:
+    def __init__(self, split, where, row, beside, chunks, sems):
+        self.split, self.where, self.row, self.beside = split, where, row, beside
+        self.chunks, self.sems = chunks, sems
+        self.started, self.first, self.second, self.third, self.core = [], {}, {}, {}, {}
+        self.step = 0
+
+    def launch(self, copy):
+        copy.start()
+        self.started.append(copy)
+        return copy
+
+    def rows(self, i, y, x, c):
+        _, ny, nx, nc = self.split
+        _, full, per, low, count, _, _ = self.chunks[i]
+        slot = ((y * nx) + x) * nc + c
+        return pl.ds(pl.multiple_of(slot * per + low, TILE_ROWS), count)
+
+    def block(self, i, y, x, c, half=None):
+        full, low, count, start, width = (self.chunks[i][k] for k in (1, 3, 4, 5, 6))
+        rows, cols = self.rows(i, y, x, c), pl.ds(start, width)
+        if half is not None and width % (2 * LANES) == 0:
+            cols = pl.ds(start + half * (width // 2), width // 2)
+        elif half is not None:
+            slot = ((y * self.split[2]) + x) * self.split[3] + c
+            at = slot * self.chunks[i][2] + low + half * (count // 2)
+            rows = pl.ds(pl.multiple_of(at, TILE_ROWS), count // 2)
+        return full.at[:, rows, cols]
+
+    def spread(self, i):
+        z, y, x, c = self.where
+        shard, full, _, low, count, start, width = self.chunks[i]
+        row_send, row_recv = self.sems[0], self.sems[1]
+        own = full.at[z, self.rows(i, y, x, c), pl.ds(start, width)]
+        mine = shard.at[pl.ds(low, count), pl.ds(start, width)]
+        self.first[i] = [
+            self.launch(remote(mine, own, row_send.at[i, k], row_recv.at[i, k], device))
+            for k, device in enumerate(self.row)
         ]
-        return [
-            lax.psum_scatter(
-                item.astype(jnp.bfloat16), "frame", scatter_dimension=0, tiled=True
-            ).astype(jnp.float32)
-            for item in fold_rows(received)
+        keep = pltpu.make_async_copy(mine, own, self.sems[6].at[i])
+        keep.start()
+        self.first[i].append(keep)
+
+    def side(self, i, k, block, device):
+        return self.launch(remote(block, block, self.sems[2].at[i, k], self.sems[3].at[i, k], device))
+
+    def to_twin(self, i, k, block):
+        twin = self.beside[2]
+        return self.launch(remote(block, block, self.sems[4].at[i, k], self.sems[5].at[i, k], twin))
+
+    def sideways(self, i):
+        _, y, x, c = self.where
+        for copy in self.first[i][:-1]:
+            copy.wait_recv()
+        self.first[i][-1].wait()
+        block = self.block(i, y, x, c)
+        self.second[i] = [self.side(i, k, block, self.beside[k]) for k in range(2)]
+        self.core[i] = [self.to_twin(i, 0, block)]
+
+    def relay(self, i):
+        _, y, x, c = self.where
+        self.second[i][0].wait_recv()
+        self.third[i] = [self.side(i, 2, self.block(i, y, 1 - x, c, 0), self.beside[1])]
+        self.core[i].append(self.to_twin(i, 1, self.block(i, y, 1 - x, c)))
+        self.second[i][1].wait_recv()
+        self.third[i].append(self.side(i, 3, self.block(i, 1 - y, x, c, 1), self.beside[0]))
+        self.core[i].append(self.to_twin(i, 2, self.block(i, 1 - y, x, c)))
+
+    def finish(self, i):
+        _, y, x, c = self.where
+        for copy in self.third[i]:
+            copy.wait_recv()
+        self.core[i].append(self.to_twin(i, 3, self.block(i, 1 - y, 1 - x, c)))
+
+    def receive(self, i):
+        for copy in self.core[i]:
+            copy.wait_recv()
+
+    def begin(self, ahead):
+        self.ahead = ahead
+        for i in range(ahead):
+            self.spread(i)
+
+    def advance(self):
+        t, count = self.step, len(self.chunks)
+        self.step += 1
+        if t < count:
+            self.sideways(t)
+        if t + self.ahead < count:
+            self.spread(t + self.ahead)
+        if 0 <= t - 2 < count:
+            self.finish(t - 2)
+        if 0 <= t - 3 < count:
+            self.receive(t - 3)
+        if 0 <= t - 1 < count:
+            self.relay(t - 1)
+
+    def end(self):
+        for copy in self.started:
+            copy.wait_send()
+
+
+class Totals:
+    def __init__(self, split, where, row, beside, count, bufs, sems, put):
+        self.split, self.where, self.row, self.beside, self.count = split, where, row, beside, count
+        self.staged, self.held, self.low, self.high, self.from_x, self.from_y, self.from_row = bufs
+        self.sems, self.put = sems, put
+        self.core, self.diagonal, self.aside, self.last = {}, {}, {}, {}
+        self.folded = self.crossed = self.joined = self.done = self.swapped = 0
+
+    def room(self, u):
+        while self.folded < u - STAGES + 1:
+            self.fold_core(self.folded)
+        if u >= STAGES:
+            self.core[u - STAGES].wait_send()
+
+    def each_row(self, act):
+        each(self.split[0], act)
+
+    def swap(self, u):
+        c = self.where[3]
+        if u >= RING:
+            while self.done < u - RING + 1:
+                self.turn()
+            pl.semaphore_wait(self.sems[6].at[u - RING], len(self.row) + len(self.beside))
+        block = self.staged.at[u % STAGES, :, :, :, 1 - c]
+        self.core[u] = remote(
+            block, self.held.at[u % RING], self.sems[0].at[u], self.sems[1].at[u], self.beside[2]
+        )
+        self.core[u].start()
+        self.swapped = u + 1
+
+    def side(self, u, k, block, target, device):
+        copy = remote(block, target, self.sems[2].at[u, k], self.sems[3].at[u, k], device)
+        copy.start()
+        return copy
+
+    def fold_core(self, u):
+        _, y, x, c = self.where
+        s, q = u % RING, u % STAGES
+        held, half = self.held, TILE // 2
+        self.core[u].wait_recv()
+
+        def fold(yy, xx):
+            def act(k):
+                held[s, k, yy, xx] = held[s, k, yy, xx] + self.staged[q, k, yy, xx, c]
+
+            self.each_row(act)
+
+        fold(1 - y, 1 - x)
+        low = held.at[s, :, 1 - y, 1 - x, :, pl.ds(0, half)]
+        high = held.at[s, :, 1 - y, 1 - x, :, pl.ds(half, half)]
+        self.diagonal[u] = [
+            self.side(u, 0, low, self.low.at[s], self.beside[0]),
+            self.side(u, 1, high, self.high.at[s], self.beside[1]),
         ]
-    devices = split[0] * split[1] * split[2] * split[3]
-    wide = [k for k, item in enumerate(terms) if item.ndim == 2]
-    thin = [k for k, item in enumerate(terms) if item.ndim == 1]
-    low = [item.astype(jnp.bfloat16) for item in terms]
-    order = wide[::-1]
-    sums = sum_shards(split, [low[k] for k in order] + [pack_small([low[k] for k in thin], devices)])
-    vectors = unpack_small(sums[-1], [terms[k].shape[0] // devices for k in thin])
-    result = dict(zip(order, sums[:-1])) | dict(zip(thin, vectors))
-    return [result[k] for k in range(len(terms))]
+        fold(1 - y, x)
+        fold(y, 1 - x)
+        fold(y, x)
+        self.folded = u + 1
+
+    def fold_diagonal(self, u):
+        _, y, x, _ = self.where
+        s, held, half = u % RING, self.held, TILE // 2
+        self.diagonal[u][0].wait_recv()
+
+        def act_low(k):
+            held[s, k, 1 - y, x, :, :half] = held[s, k, 1 - y, x, :, :half] + self.low[s, k]
+
+        self.each_row(act_low)
+        block = held.at[s, :, 1 - y, x]
+        self.aside[u] = [self.side(u, 2, block, self.from_y.at[s], self.beside[1])]
+        self.diagonal[u][1].wait_recv()
+
+        def act_high(k):
+            held[s, k, y, 1 - x, :, half:] = held[s, k, y, 1 - x, :, half:] + self.high[s, k]
+
+        self.each_row(act_high)
+        block = held.at[s, :, y, 1 - x]
+        self.aside[u].append(self.side(u, 3, block, self.from_x.at[s], self.beside[0]))
+        self.crossed = u + 1
+
+    def fold_side(self, u):
+        z, y, x, _ = self.where
+        s, held, depth = u % RING, self.held, self.split[0]
+        for copy in self.aside[u]:
+            copy.wait_recv()
+
+        def act(k):
+            total = held[s, k, y, x].astype(WIDE) + self.from_x[s, k].astype(WIDE)
+            held[s, k, y, x] = (total + self.from_y[s, k].astype(WIDE)).astype(LOW)
+
+        self.each_row(act)
+        self.last[u] = []
+        for k, device in enumerate(self.row):
+            copy = remote(
+                held.at[s, (z + k + 1) % depth, y, x],
+                self.from_row.at[s, k],
+                self.sems[4].at[u, k],
+                self.sems[5].at[u, k],
+                device,
+            )
+            copy.start()
+            self.last[u].append(copy)
+        self.joined = u + 1
+
+    def fold_row(self, u):
+        z, y, x, _ = self.where
+        s = u % RING
+        for copy in self.last[u]:
+            copy.wait_recv()
+        total = self.held[s, z, y, x].astype(WIDE)
+        for k in range(self.split[0] - 1):
+            total = total + self.from_row[s, k].astype(WIDE)
+        self.put(u, total)
+        for copy in self.diagonal[u] + self.aside[u] + self.last[u]:
+            copy.wait_send()
+        if u + RING < self.count:
+            for device in self.row + list(self.beside):
+                pl.semaphore_signal(self.sems[6].at[u], inc=1, device_id=device, device_id_type=MESH)
+        self.done = u + 1
+
+    def turn(self):
+        row, side, cross, core = self.joined, self.crossed, self.folded, self.swapped
+        if self.done < row:
+            self.fold_row(self.done)
+        if self.joined < side:
+            self.fold_side(self.joined)
+        if self.crossed < cross:
+            self.fold_diagonal(self.crossed)
+        if self.folded < core:
+            self.fold_core(self.folded)
+
+    def end(self):
+        while self.done < self.count:
+            self.turn()
+        for u in range(max(self.count - STAGES, 0), self.count):
+            self.core[u].wait_send()
+
+
+def pairs_kernel(split, shape, *refs):
+    frames, groups, valid, block = shape
+    it = iter(refs)
+    take = lambda n: [next(it) for _ in range(n)]
+    (x_in, dy_in, small_in), shards = take(3), take(7)
+    out_ref, grad_ref = take(2)
+    g_t_in, g_t_out, g_t_lin, g_s_in, g_s_out, g_up, g_down, g_small = take(8)
+    small_all, full = next(it), take(7)
+    xt, a_t, z_t, p_t, o_t, u_t, dy, x1, x2, a_s, z_s, p_s, o_s, a_m, act_g, slope, acc, at, low = take(19)
+    b_recv, db_recv, dt_recv, sent, vec, sums, small_v, tile_v = take(8)
+    w_a, w_b, w_up, w_down = take(4)
+    bufs = take(7)
+    ag_sems, rs_sems = take(7), take(7)
+    ex_send, ex_recv, ex_own, load_sem, misc = take(5)
+
+    where, row, beside = place(split)
+    z, y, x, c = where
+    nz, ny, nx, nc = split
+    corner = (z * ny + y, (1 - x) * nc + (1 - c))
+    greet(row + list(beside) + [corner])
+    rows, width = x1.shape
+    span = rows // frames
+    pair = 2 * block
+    chunk = pair
+    mine = x * nc + c
+    peers = [(beside[0], (1 - x) * nc + c), (beside[2], x * nc + (1 - c)), (corner, (1 - x) * nc + (1 - c))]
+    waiting = []
+
+    def cut(ref, index):
+        if len(ref.shape) == 3:
+            return ref.at[index]
+        return ref.at[pl.ds(pl.multiple_of(index * block, TILE_ROWS), block)]
+
+    def exchange(e, source, target, to_places):
+        copies = []
+        for f in range(frames):
+            for k, (device, index) in enumerate(peers):
+                src = f * groups + index if to_places else index * frames + f
+                dst = mine * frames + f if to_places else f * groups + mine
+                copy = remote(cut(source, src), cut(target, dst), ex_send.at[e, k, f], ex_recv.at[e, k, f], device)
+                copy.start()
+                copies.append(copy)
+            src = f * groups + mine if to_places else mine * frames + f
+            dst = mine * frames + f if to_places else f * groups + mine
+            own = pltpu.make_async_copy(cut(source, src), cut(target, dst), ex_own.at[e, f])
+            own.start()
+            copies.append(own)
+        return copies
+
+    def arrive(copies):
+        for copy in copies:
+            copy.wait()
+
+    moved = exchange(0, x_in, xt, True)
+    dims = [s.shape for s in shards]
+    chunks = [(small_in, small_all, SMALL_ROWS, 0, SMALL_ROWS, 0, LANES)]
+    for k in (0, 1, 2, 3, 4):
+        chunks.append((shards[k], full[k], dims[k][0], 0, dims[k][0], 0, dims[k][1]))
+    half = dims[5][1] // 2
+    for k in range(2):
+        chunks.append((shards[5], full[5], dims[5][0], 0, dims[5][0], k * half, half))
+    half = dims[6][0] // 2
+    for k in range(2):
+        chunks.append((shards[6], full[6], dims[6][0], k * half, half, 0, dims[6][1]))
+    ag = Gather(split, where, row, beside, chunks, ag_sems)
+    ag.begin(2)
+    loads = {}
+
+    def load(key, source, target):
+        copy = pltpu.make_async_copy(source, target, load_sem.at[len(loads)])
+        copy.start()
+        loads[key] = copy
+
+    load("dy", dy_in, dy)
+    load("x", x_in, low)
+    sums[...] = jnp.zeros_like(sums)
+    wb = [w_b.at[:, :, pl.ds(k * width, width)] for k in range(3)]
+    wa = w_a
+    for _ in range(4):
+        ag.advance()
+    load("small", small_all, small_v)
+    loads["small"].wait()
+    devices = nz * ny * nx * nc
+    per_row = devices * SMALL_ROWS // (nz * SMALL_ROWS)
+
+    def small_of(r):
+        k, s = r // per_row, r % per_row
+        tile = small_v[k, s * SMALL_ROWS : (s + 1) * SMALL_ROWS, :].astype(WIDE)
+        return jnp.concatenate([tile, jnp.zeros((SMALL_ROWS, width - LANES), WIDE)], axis=1)
+
+    parts = {}
+
+    def add(key, value):
+        parts[key] = parts[key] + value if key in parts else value
+
+    step = width // devices
+    for r in range(devices):
+        tile = small_of(r)
+        add("a", pltpu.roll(tile, r * step, 1) if r else tile)
+        for name, times in (("b", 2), ("c", 4)):
+            at_row, at_col = r * step * times // width, r * step * times % width
+            add((name, at_row), pltpu.roll(tile, at_col, 1) if at_col else tile)
+    vec[0:10, :] = parts["a"][0:10]
+    for k in range(2):
+        vec[T_INB + k : T_INB + k + 1, :] = parts["b", k][10:11]
+        vec[S_INB + k : S_INB + k + 1, :] = parts["b", k][11:12]
+    for k in range(4):
+        vec[E_BIAS + k : E_BIAS + k + 1, :] = parts["c", k][12:13]
+
+    arrive(moved)
+    norm_stage(xt, vec, T_GAIN, a_t, chunk)
+    ag.advance()
+    load("t_in", full[0], wa)
+    loads["t_in"].wait()
+    inproj_stage(a_t, wa, vec, T_INB, z_t)
+    ag.advance()
+    load("t_out", full[1], wb[0])
+    all_frames = frames * groups
+    time_attend(z_t, p_t, o_t, all_frames, block, 0, all_frames // 4)
+    ag.advance()
+    load("t_lin", full[2], wb[1])
+    time_attend(z_t, p_t, o_t, all_frames, block, all_frames // 4, all_frames // 2)
+
+    def store(ref):
+        def act(cols, total):
+            if len(ref.shape) == 3:
+                ref[:, :, cols] = total.reshape(ref.shape[:2] + (-1,)).astype(LOW)
+            else:
+                ref[:, cols] = total.astype(LOW)
+
+        return act
+
+    loads["t_out"].wait()
+    project_stage(o_t, wb[0], vec, T_OUTB, store(u_t))
+    loads["t_lin"].wait()
+    project_stage(u_t, wb[1], vec, T_LINB, store(sent))
+    moved = exchange(1, sent, b_recv, False)
+    ag.advance()
+    load("s_in", full[3], wa)
+    loads["x"].wait()
+    arrive(moved)
+
+    def first(k):
+        r = tiles(k, chunk)
+        x1[r, :] = low[r, :].astype(WIDE) + wide_rows(b_recv, k, chunk)
+
+    each(rows // chunk, first)
+    norm_stage(x1, vec, S_GAIN, a_s, chunk)
+    loads["s_in"].wait()
+    inproj_stage(a_s, wa, vec, S_INB, z_s)
+    ag.advance()
+    load("s_out", full[4], wb[2])
+    heads = width // LANES * frames
+    space_attend(z_s, p_s, o_s, frames, span, valid, block, 0, heads // 2)
+    ag.advance()
+    half = w_up.shape[2] // 2
+    load("up0", full[5].at[:, :, pl.ds(0, half)], w_up.at[:, :, pl.ds(0, half)])
+    space_attend(z_s, p_s, o_s, frames, span, valid, block, heads // 2, heads)
+
+    def add_x1(cut, total):
+        x2[:, cut] = x1[:, cut] + total
+
+    loads["s_out"].wait()
+    project_stage(o_s, wb[2], vec, S_OUTB, add_x1)
+    norm_stage(x2, vec, F_GAIN, a_m, chunk)
+    ag.advance()
+    load("up1", full[5].at[:, :, pl.ds(half, half)], w_up.at[:, :, pl.ds(half, half)])
+    loads["up0"].wait()
+    expand_stage(a_m, w_up, vec, act_g, slope, 0, half // TILE)
+    ag.advance()
+    loads["up1"].wait()
+    expand_stage(a_m, w_up, vec, act_g, slope, half // TILE, 2 * half // TILE)
+    loads["dy"].wait()
+
+    per = width // TILE
+    plan = {}
+    order = [(g_up, 4 * per), (g_s_out, per), (g_s_in, 3 * per), (g_t_lin, per), (g_t_out, per), (g_t_in, 3 * per), (g_small, 1)]
+    units, sub = per - 1, SUB
+    homes = {}
+    for out, count in order:
+        for k in range(count):
+            if sub == SUB:
+                units, sub = units + 1, 0
+                plan[units] = []
+            plan[units].append((out, k))
+            homes[id(out), k] = (units, sub)
+            sub += 1
+    count = units + 1
+    step_rows = g_up.shape[0]
+
+    def put(u, total):
+        if u < per:
+            g_down[:, u * TILE : (u + 1) * TILE] = total
+            return
+        for b, (out, k) in enumerate(plan[u]):
+            out[:, k * TILE : (k + 1) * TILE] = total[b * step_rows : (b + 1) * step_rows]
+
+    rs = Totals(split, where, row, beside, count, bufs, rs_sems, put)
+    staged = bufs[0]
+
+    def down(k):
+        at[:width, :] = act_g[:, tiles(k, width)].T
+        for u in range(per):
+            total = dot(at[:width, :], dy[:, u * TILE : (u + 1) * TILE])
+            staged[u, k] = total.reshape((ny, nx, nc, -1, TILE)).astype(LOW)
+
+    each(nz, down)
+    ones = jnp.ones((16, rows), LOW)
+    sums[R_BIAS : R_BIAS + 1, :] = dot(ones, dy[...])[:1]
+    for u in range(per):
+        rs.swap(u)
+    ag.advance()
+    load("down", full[6], w_down)
+    assert ag.step == len(chunks) + 3
+
+    def grads(out, dz_ref, table):
+        count = out.shape[1] // TILE
+        act_bias = bias_rows(sums, table, width)
+        k = 0
+        while k < count:
+            u, b0 = homes[id(out), k]
+            n = min(SUB - b0, count - k)
+            if b0 == 0:
+                rs.room(u)
+
+            def act(i, k=k, u=u, b0=b0, n=n):
+                t = k + i
+                total = dot(at[...], dz_ref[:, tiles(t)])
+                act_bias(t, total[width : width + 1])
+                tile_v[...] = total[:width]
+                for b in range(n):
+
+                    @pl.when(i == b)
+                    def _():
+                        low_row = (b0 + b) * step_rows
+                        staged[u % STAGES, :, :, :, :, low_row : low_row + step_rows, :] = (
+                            tile_v[...].reshape((nz, ny, nx, nc, step_rows, TILE)).astype(LOW)
+                        )
+
+            each(n, act)
+            k += n
+            if b0 + n == SUB:
+                rs.swap(u)
+                rs.turn()
+
+    loads["down"].wait()
+    reduce_back_stage(dy, w_down, slope, slope)
+
+    hidden = act_g.shape[1]
+    rs.turn()
+    reduce_stage(act_g, w_down, vec, x2, store(low))
+    out_copy = pltpu.make_async_copy(low, out_ref, misc.at[0])
+    out_copy.start()
+    rs.turn()
+    turn_stage(a_m, at)
+    grads(g_up, slope, [E_BIAS + k for k in range(hidden // width)])
+    back_stage(slope, w_up, acc)
+    out_copy.wait()
+
+    def put_x2(k, dv):
+        r = tiles(k, chunk)
+        total = dy[r, :].astype(WIDE) + dv
+        x2[r, :] = total
+        low[r, :] = total.astype(LOW)
+
+    norm_back_stage(x2, vec, F_GAIN, acc, sums, chunk, put_x2)
+    load("t_in again", full[0], w_up.at[:, :, pl.ds(0, 3 * width)])
+    turn_stage(o_s, at)
+    grads(g_s_out, low, [S_OUTB])
+    back_stage(low, wb[2], acc)
+    low[...] = acc[...].astype(LOW)
+    rs.turn()
+    dz = slope.at[:, pl.ds(0, 3 * width)]
+    space_attend_back(z_s, p_s, low, dz, frames, span, 0, heads // 2)
+    rs.turn()
+    space_attend_back(z_s, p_s, low, dz, frames, span, heads // 2, heads)
+    rs.turn()
+    back_stage(dz, wa, acc)
+
+    def put_x1(k, dv):
+        r = tiles(k, chunk)
+        total = x2[r, :] + dv
+        x1[r, :] = total
+        put_rows(sent, k, chunk, total)
+
+    norm_back_stage(x1, vec, S_GAIN, acc, sums, chunk, put_x1)
+    moved = exchange(2, sent, db_recv, True)
+    turn_stage(a_s, at)
+    grads(g_s_in, dz, [S_INB, None, S_INB + 1])
+    turn_stage(u_t, at)
+    arrive(moved)
+
+    def flat(k):
+        low[tiles(k, chunk), :] = wide_rows(db_recv, k, chunk).astype(LOW)
+
+    each(rows // chunk, flat)
+    grads(g_t_lin, low, [T_LINB])
+    back_stage(low, wb[1], acc)
+    low[...] = acc[...].astype(LOW)
+    rs.turn()
+    turn_stage(o_t, at)
+    grads(g_t_out, low, [T_OUTB])
+    back_stage(low, wb[0], acc)
+    low[...] = acc[...].astype(LOW)
+    rs.turn()
+    time_attend_back(z_t, p_t, low, dz, x2, acc, all_frames, block, rs.turn)
+    loads["t_in again"].wait()
+    back_stage(dz, w_up.at[:, :, pl.ds(0, 3 * width)], acc)
+
+    def put_t(k, dv):
+        put_rows(sent, k, chunk, dv)
+
+    norm_back_stage(xt, vec, T_GAIN, acc, sums, chunk, put_t)
+    moved = exchange(3, sent, dt_recv, False)
+    rs.turn()
+    turn_stage(a_t, at)
+    grads(g_t_in, dz, [T_INB, None, T_INB + 1])
+
+    u, b0 = homes[id(g_small), 0]
+    if b0 == 0:
+        rs.room(u)
+    low_row = b0 * step_rows
+    lane = lax.broadcasted_iota(jnp.int32, (step_rows, width), 0)
+    base = jnp.concatenate([sums[0:10, :], jnp.zeros((step_rows - 10, width), WIDE)], axis=0)
+
+    def placed(pieces):
+        out = jnp.zeros((step_rows, width), WIDE)
+        for target, source in pieces:
+            out = jnp.where(lane == target, sums[source : source + 1, :], out)
+        return out
+
+    twos = [placed([(10, T_INB + k), (11, S_INB + k)]) for k in range(2)]
+    fours = [placed([(12, E_BIAS + k)]) for k in range(4)]
+    for r in range(devices):
+        def shifted(value, at_col):
+            return (pltpu.roll(value, width - at_col, 1) if at_col else value)[:, :TILE]
+
+        a = shifted(base, r * step)
+        b = shifted(twos[2 * r * step // width], 2 * r * step % width)
+        d = shifted(fours[4 * r * step // width], 4 * r * step % width)
+        tile = jnp.where(lane[:, :TILE] < 10, a, jnp.where(lane[:, :TILE] < 12, b, d))
+        slot = (r // (ny * nx * nc), r // (nx * nc) % ny, r // nc % nx, r % nc)
+        staged[(u % STAGES,) + slot + (slice(low_row, low_row + step_rows), slice(None))] = tile.astype(LOW)
+    rs.swap(u)
+    rs.turn()
+    arrive(moved)
+
+    def last(k):
+        r = tiles(k, chunk)
+        x1[r, :] = x1[r, :] + wide_rows(dt_recv, k, chunk)
+
+    each(rows // chunk, last)
+    grad_copy = pltpu.make_async_copy(x1, grad_ref, misc.at[1])
+    grad_copy.start()
+    rs.end()
+    ag.end()
+    grad_copy.wait()
+
+
+def whole_layer(split, shape, x, dy, small, shards):
+    frames, groups, valid, block = shape
+    rows, width = x.shape
+    nz, ny, nx, nc = split
+    slots = ny * nx * nc
+    low, wide = LOW, WIDE
+    hidden = shards[5].shape[1]
+    step = shards[0].shape[0]
+    shapes = [(item.shape, wide) for item in shards] + [((step, TILE), wide)]
+    token, full = ((rows, width), low), ((rows, width), wide)
+    gathered = [((nz, slots * SMALL_ROWS, LANES), low)]
+    gathered += [((nz, slots * item.shape[0], item.shape[1]), low) for item in shards]
+    hbm = pl.BlockSpec(memory_space=pl.ANY)
+    vmem = pl.BlockSpec(memory_space=pltpu.VMEM)
+    outs = [token, full] + shapes + gathered
+    out_specs = [hbm, hbm] + [vmem] * len(shapes) + [hbm] * len(gathered)
+    span = rows // frames
+    three, big = ((rows, 3 * width), low), ((rows, hidden), low)
+    cuts = ((frames * groups, block, width), low)
+    scratch = [cuts, token, three, ((frames * groups, rows, LANES), low), token, token, token, full, full]
+    scratch += [token, three, ((frames * HEADS, span, span), low), token, token, big, big, full]
+    scratch += [((width + 16, rows), low), token, cuts, cuts, cuts, cuts, ((24, width), wide), ((24, width), wide)]
+    scratch += [gathered[0], ((width, TILE), wide)]
+    scratch += [gathered[1], gathered[1], gathered[6], gathered[7]]
+    deep = SUB * step
+    scratch += [((STAGES, nz, ny, nx, nc, deep, TILE), low), ((RING, nz, ny, nx, deep, TILE), low)]
+    scratch += [((RING, nz, deep, TILE // 2), low)] * 2 + [((RING, nz, deep, TILE), low)] * 2
+    scratch += [((RING, nz - 1, deep, TILE), low)]
+    sem = pltpu.SemaphoreType.DMA
+    chunks, units = 10, (hidden // TILE + 5 * width * 3 // TILE) // SUB + 8
+    sems = [sem((chunks, nz - 1))] * 2 + [sem((chunks, 4))] * 4 + [sem((chunks,))]
+    sems += [sem((units,))] * 2 + [sem((units, 4))] * 2 + [sem((units, nz - 1))] * 2
+    sems += [pltpu.SemaphoreType.REGULAR((units,))]
+    sems += [sem((4, 3, frames))] * 2 + [sem((4, frames)), sem((12,)), sem((2,))]
+    result = pl.pallas_call(
+        functools.partial(pairs_kernel, split, shape),
+        out_shape=[jax.ShapeDtypeStruct(s, kind) for s, kind in outs],
+        in_specs=[hbm] * (3 + len(shards)),
+        out_specs=out_specs,
+        scratch_shapes=[pltpu.VMEM(s, kind) for s, kind in scratch] + sems,
+        compiler_params=pltpu.CompilerParams(
+            collective_id=0, has_side_effects=True, vmem_limit_bytes=63 << 20
+        ),
+        name="whole_layer",
+    )(x, dy, small, *shards)
+    return result[:10]
 
 
 VECTOR_ROWS = (0, 1, 10, 2, 3, 4, 5, 12, 6, 7, 8, 14, 9)
+
+
+SMALL_PLACES = {row: (row, 0) for row in range(10)} | {10: (10, 0), 12: (11, 0), 14: (12, 0)}
+
+
+def pack_small(vectors):
+    rows = {SMALL_PLACES[at][0]: item for at, item in zip(VECTOR_ROWS, vectors)}
+    lines = [jnp.pad(rows[k], (0, LANES - rows[k].shape[0])) for k in range(len(rows))]
+    lines += [jnp.zeros((LANES,), LOW)] * (SMALL_ROWS - len(lines))
+    return jnp.stack(lines)
+
+
+def sum_native(terms):
+    received = [
+        lax.all_to_all(
+            item.astype(LOW), "clip", split_axis=0, concat_axis=0, tiled=True
+        ).astype(WIDE)
+        for item in stack_rows(terms, lax.axis_size("clip"))
+    ]
+    return [
+        lax.psum_scatter(item.astype(LOW), "frame", scatter_dimension=0, tiled=True).astype(WIDE)
+        for item in fold_rows(received)
+    ]
 
 
 def on_device(
@@ -888,7 +1311,6 @@
         reduce_weight,
         reduce_bias,
     ]
-    full = gather_all(split, params)
     frames, places, width = video_tokens.shape[1:]
     groups = lax.axis_size("frame")
     valid = places // groups
@@ -924,6 +1346,28 @@
     def weight(item):
         return item.reshape((4, -1, item.shape[1]))
 
+    if split is not None:
+        small = pack_small([item for item in params if item.ndim == 1])
+        layer_out, input_grad, *sums = whole_layer(
+            split,
+            (frames, groups, valid, block),
+            padded(video_tokens).reshape((rows, width)),
+            padded(cotangent).reshape((rows, width)),
+            small,
+            [item for item in params if item.ndim == 2],
+        )
+        wide, thin = iter(sums[:7]), iter(zip(VECTOR_ROWS, [item for item in params if item.ndim == 1]))
+        summed = []
+        for item in params:
+            if item.ndim == 2:
+                summed.append(next(wide))
+            else:
+                at, like = next(thin)
+                row, _ = SMALL_PLACES[at]
+                summed.append(sums[7][row, : like.shape[0]])
+        return (trimmed(layer_out), trimmed(input_grad)) + tuple(summed)
+
+    full = [lax.all_gather(item, ("clip", "frame"), axis=0, tiled=True) for item in params]
     thin = [item for item in full if item.ndim == 1]
     t_in, t_out, t_lin, s_in, s_out, w_up, w_down = [weight(item) for item in full if item.ndim == 2]
     pieces = sorted(zip(VECTOR_ROWS, thin), key=lambda pair: pair[0])
@@ -962,7 +1406,7 @@
             at = next(rows_of)
             count = item.shape[0] * lax.axis_size(("clip", "frame")) // width
             terms.append(sums[at : at + count].reshape(-1))
-    summed = sum_all(split, terms)
+    summed = sum_native(terms)
     return (trimmed(layer_out), trimmed(input_grad)) + tuple(summed)
 
 

time: 398 us -> 283 us (0.71)
  Pallas kernels: 335 us -> 258 us
  waiting for transfers between devices: 17.1 us -> 0 us
  starting transfers between devices: 15.8 us -> 0 us
    pallas_call x5 -> x1, Pallas kernels: 335 us -> 258 us  [whole_layer(): pl.pallas_call(functools.partial(pairs_kernel, split, shape), out_shape=[...]
    all_to_all x4 -> x0, waiting for transfers between devices: 17.1 us -> none  [the longest x2 8.89 us: to_places(): lax.all_to_all(tokens.reshape((frames, groups, block, width)), 'frame', s...]
    all_to_all x4 -> x0, starting transfers between devices: 15.8 us -> none  [the longest x2 7.91 us: to_places(): lax.all_to_all(tokens.reshape((frames, groups, block, width)), 'frame', s...]
    another operation x13 -> x10, local copies, waits for them, and re-layouts: 1.2 us -> 5.99 us  [pack_small(): return jnp.stack(lines)]
    reshape x5 -> x0, local copies, waits for them, and re-layouts: 4.47 us -> none  [the longest x1 2.08 us: to_places(): tokens.reshape((frames, groups, block, width))]
    unnamed x62 -> x23, local copies, waits for them, and re-layouts: 9.01 us -> 4.73 us
    squeeze x0 -> x3, local copies, waits for them, and re-layouts: none -> 4.01 us  [on_device(): summed.append(sums[7][row, :like.shape[0]])]
  transfers between devices with their start and end apart: 4 -> 0, of which waited for: 2 -> 0; matrix products, arithmetic and copies ran while one was open for 3% -> 0% of each run, Pallas kernels for 54% -> 0%
where the time goes in v1:
time: 283 us
  Pallas kernels  258 us (91%)
  local copies, waits for them, and re-layouts  23.7 us (8%)
    pallas_call x1, Pallas kernels, whole_layer(): pl.pallas_call(functools.partial(pairs_kernel, split, shape), out_shape=[...  258 us
    another operation x10, local copies, waits for them, and re-layouts, pack_small(): return jnp.stack(lines)  5.99 us
    slice x2, local copies, waits for them, and re-layouts, trimmed(): cut = tokens.reshape((frames, groups, block, width))[:, :, :valid]  5.91 us

profile of v1, /device:TPU:0, one launch (start us, length us, event | category | flops | bytes accessed | tf_op | source)
XLA Modules:
  0.0 282.6 jit_solution(9811379294163174821)
XLA Ops:
  0.7 0.7 pad_bitcast_fusion.12
  1.4 0.7 pad_bitcast_fusion.10
  2.1 0.7 pad_bitcast_fusion.2
  2.7 0.7 pad_bitcast_fusion.8
  3.4 0.7 pad_bitcast_fusion.6
  4.1 0.7 pad_bitcast_fusion
  4.8 0.7 pad_bitcast_fusion.4
  5.5 1.2 stack.59.refs_2_
  6.7 1.1 copy.44
  7.8 0.9 pad.49
  8.8 0.9 pad.50
  9.7 258.2 %whole_layer.1 = (bf16[448,768]{1,0:T(8,128)(2,1)}, f32[448,768]{1,0:T(8,128)}, f32[24,2304]{1,0:T(8,128)}, f32[24,768]{1,0:T(8,128)}, f32[24,768]{1,0:T(8,128)}...) custom-call(bf16[448,768]{1,0:T(8,128)(2,1)} %bitcast.62, ...), custom_call_target="tpu_custom_call" | custom-call | tf_op jit(solution)/shard_map/whole_layer/pallas_call | solution.py:1227
  267.9 2.5 copy.46
  270.5 3.4 %copy.47 = f32[2,4,49,768]{3,0,2,1:T(2,128)} copy(f32[2,4,49,768]{3,2,1,0:T(8,128)} %bitcast.64) | data formatting | bytes 2408448 | tf_op jit(solution)/shard_map/slice | solution.py:1343
  273.8 1.2 slice_bitcast_fusion.1
  275.1 1.3 slice_bitcast_fusion.5
  276.3 1.5 slice_bitcast_fusion
  277.9 0.7 copy.55
  278.5 0.6 copy.56
  279.2 0.6 copy.57
  279.8 0.7 copy.58
  280.5 0.6 copy.59
  281.1 0.7 copy.60
  281.9 0.7 copy.61
  (19 shorter events, 0.1 us)
Async XLA Ops:
  0.7 8.0 %copy-start = (bf16[1,2,196,768]{3,1,2,0:T(2,128)(2,1)S(1)}, bf16[1,2,196,768]{3,1,2,0:T(2,128)(2,1)}, u32[]{:S(2)}) copy-start(bf16[1,2,196,768]{3,1,2,0:T(2,128)(2,1)} %param.43) | copy-start | bytes 1806340
  270.4 7.4 %copy-start.4 = (f32[24,2304]{1,0:T(8,128)S(1)}, f32[24,2304]{1,0:T(8,128)}, u32[]{:S(2)}) copy-start(f32[24,2304]{1,0:T(8,128)} %get-tuple-element.92) | copy-start | bytes 663556
  270.4 8.1 %copy-start.7 = (f32[24,768]{1,0:T(8,128)S(1)}, f32[24,768]{1,0:T(8,128)}, u32[]{:S(2)}) copy-start(f32[24,768]{1,0:T(8,128)} %get-tuple-element.94) | copy-start | bytes 221188
  270.4 8.7 %copy-start.6 = (f32[24,768]{1,0:T(8,128)S(1)}, f32[24,768]{1,0:T(8,128)}, u32[]{:S(2)}) copy-start(f32[24,768]{1,0:T(8,128)} %get-tuple-element.96) | copy-start | bytes 221188
  270.4 9.4 %copy-start.3 = (f32[24,2304]{1,0:T(8,128)S(1)}, f32[24,2304]{1,0:T(8,128)}, u32[]{:S(2)}) copy-start(f32[24,2304]{1,0:T(8,128)} %get-tuple-element.100) | copy-start | bytes 663556
  270.4 10.1 %copy-start.5 = (f32[24,768]{1,0:T(8,128)S(1)}, f32[24,768]{1,0:T(8,128)}, u32[]{:S(2)}) copy-start(f32[24,768]{1,0:T(8,128)} %get-tuple-element.102) | copy-start | bytes 221188
  270.5 10.7 %copy-start.2 = (f32[24,3072]{1,0:T(8,128)S(1)}, f32[24,3072]{1,0:T(8,128)}, u32[]{:S(2)}) copy-start(f32[24,3072]{1,0:T(8,128)} %get-tuple-element.106) | copy-start | bytes 884740
  273.8 8.0 %copy-start.1 = (f32[96,768]{1,0:T(8,128)S(1)}, f32[96,768]{1,0:T(8,128)}, u32[]{:S(2)}) copy-start(f32[96,768]{1,0:T(8,128)} %get-tuple-element.108) | copy-start | bytes 884740
